TPU v7x, 32 devices: a whole 2x2x4 slice. The times are simulated.
32 devices in a mesh: parts: 2 (over y), att: 4 (over x, core), ffn: 4 (over z).
Axes of the slice: x: 2, y: 2, z: 4, core: 2. Of those that a mesh axis runs over, the one named last changes fastest.
Arguments:
- incoming: bfloat16 [128, 2, 8192], P('parts', None, 'att'), parts along dimension 0, may hold values from -60 to 60
- queries: bfloat16 [128, 2, 8192], P(('parts', 'att'), None, 'ffn'), parts along dimension 0, may hold values from -19 to 19
- new_kv: bfloat16 [128, 2, 2048], P(('parts', 'att'), None, 'ffn'), parts along dimension 0, may hold values from -6 to 6
- cache: bfloat16 [128, 640, 2048], P(('parts', 'att'), None, 'ffn'), parts along dimension 0, may hold values from -6 to 6
- lengths: int32 [128], P(('parts', 'att')), parts along dimension 0, may hold values from 1 to 640, 20480 in all
- slot_of: int32 [128], P('parts'), parts along dimension 0, may hold values from 0 to 63, each once
- w_out: bfloat16 [8192, 8192], P('ffn', 'att'), may hold values from -0.0625 to 0.0625
- norm_gain: float32 [8192], P('att'), may hold values from 0.5 to 1.5
- w_gate: bfloat16 [8192, 14336], P('att', 'ffn'), may hold values from -0.0625 to 0.0625
- w_up: bfloat16 [8192, 14336], P('att', 'ffn'), may hold values from -0.0625 to 0.0625
- w_down: bfloat16 [14336, 8192], P('ffn', 'att'), may hold values from -0.046875 to 0.046875
Outputs:
- out: bfloat16 [128, 2, 8192], P(('parts', 'ffn'), None, 'att'), parts along dimension 0
There are 2 independent parts, one for each index of `parts`. A program takes and returns all parts, laid end to end along the dimension named above; an argument that names none is the same for every part. Nothing has to cross between parts.
Inputs may be any that keep to these rules, and one draw needn't show every extreme that they name: In each part, the kept lengths of that part's 64 slots sum to 20480. `slot_of`: in each part, every slot holds exactly one request.
All inputs are finite; a program needn't handle non-finite values. No bound on the sum of `lengths` on one device may be relied on, other than what follows from the above.
Results may differ from a plain program's by a relative error of at most 0.0095.
Values may be sent and summed in bfloat16 or wider, within the bound.
A program may use at most 128 MiB of HBM per device.

v0:
```python
import functools

import jax
import jax.numpy as jnp
from jax import lax
from jax.experimental import pallas as pl
from jax.experimental.pallas import tpu as pltpu
from jax.sharding import PartitionSpec as P

D = 8192
H = 64
KVH = 8
HD = 128
STEPS = 2
CAP = 640


epsilon = 1e-05
TILE = 512
MESH = pl.DeviceIdType.MESH


def layer_kernel(
    cfg, holders, slots_row, lengths, q, kv, incoming, gain, cache, wo, wg, wu, wd, out,
    place, kept_in, gq, gkv, of, tb, attended,
    wo_v, wg_v, wu_v, wd_v,
    fa, pa, ra, sm, rm, om, res, h, ss, ssr,
    fg, s1, o1, r1, s2, o2, r2, hb,
    pd, od, rd,
    wo_s, wg_s, wu_s, wd_s,
    in_s, a_ss, a_rs, m_ss, m_rs, g_ss, g_rs, n_ss, n_rs, f_ss, f_rs, q_ss, q_rs,
    c1_ss, c1_rs, c2_ss, c2_rs,
    hp_ss, hp_rs, hx_ss, hx_rs, hf_ss, hf_rs,
    d_ss, d_rs,
    cache_s, qp_ss, qp_rs, qx_ss, qx_rs, qf_ss, qf_rs,
    tp_ss, tp_rs, tx_ss, tx_rs, tf_ss, tf_rs,
):
    Z, RB, T, NA, NF = cfg
    S = cache.shape[0]
    kv_local = cache.shape[2] // (2 * HD)
    groups = H // KVH
    QR = STEPS * groups
    per = wd_v.shape[1] // CAP
    A = 4
    z = lax.axis_index("ffn")
    a = lax.axis_index("att")
    x, c = a // 2, a % 2
    partner = 2 * x + (1 - c)
    xpeer = 2 * (1 - x) + c
    bf, f32 = jnp.bfloat16, jnp.float32

    def wcopy(src, dst, sem, k):
        return pltpu.make_async_copy(
            src.at[:, pl.ds(pl.multiple_of(k * T, T), T)], dst.at[k], sem.at[k]
        )

    def kept_rows(i):
        return pl.ds(pl.multiple_of((i % per) * CAP, CAP), CAP)

    def cache_copy(i):
        return pltpu.make_async_copy(cache.at[i], wd_v.at[i // per, kept_rows(i)], cache_s.at[i])

    @pl.loop(0, S)
    def _(i):
        cache_copy(i).start()

    half = z // 2
    in_copy = pltpu.make_async_copy(
        incoming.at[pl.ds(half * kept_in.shape[0], kept_in.shape[0])], kept_in, in_s.at[0]
    )
    in_copy.start()
    for k in range(NA):
        wcopy(wo, wo_v, wo_s, k).start()
    for k in range(NF):
        wcopy(wg, wg_v, wg_s, k).start()
        wcopy(wu, wu_v, wu_s, k).start()

    barrier = pltpu.get_barrier_semaphore()
    for d in range(1, Z):
        pl.semaphore_signal(barrier, 1, device_id={"ffn": (z + d) % Z}, device_id_type=MESH)
    for d in range(1, A):
        pl.semaphore_signal(barrier, 1, device_id={"att": (a + d) % A}, device_id_type=MESH)
    pl.semaphore_wait(barrier, Z - 1 + A - 1)

    def remote(src, dst, ss_, rs_, axis, peer):
        return pltpu.make_async_remote_copy(
            src_ref=src, dst_ref=dst, send_sem=ss_, recv_sem=rs_,
            device_id={axis: peer}, device_id_type=MESH,
        )

    inside = z * (Z - 1 - z)
    inner = 1 + half
    outer = 3 * (z - 1)
    other = 3 - z

    def half_of(ref, k, which):
        return ref.at[k, which]

    def a_copy(k, peer):
        return remote(pa.at[k], ra.at[k], a_ss.at[k], a_rs.at[k], "ffn", peer)

    def m_copy(k):
        return remote(sm.at[k], rm.at[k], m_ss.at[k], m_rs.at[k], "ffn", other)

    def g_copy(k, which):
        block = half_of(res, k, which)
        return remote(block, block, g_ss.at[k], g_rs.at[k], "ffn", other)

    def n_copy(k, which, peer):
        block = half_of(res, k, which)
        return remote(block, block, n_ss.at[k], n_rs.at[k], "ffn", peer)

    def f_copy(k, which, peer):
        block = half_of(res, k, which)
        return remote(block, block, f_ss.at[k], f_rs.at[k], "ffn", peer)

    def q_copy(d):
        peer = (a + d) % A
        return remote(ss.at[peer], ssr.at[d - 1], q_ss.at[d - 1], q_rs.at[d - 1], "att", peer)

    def c1_copy(k):
        return remote(s1.at[k], r1.at[k], c1_ss.at[k], c1_rs.at[k], "att", partner)

    def c2_copy(k):
        return remote(s2.at[k], r2.at[k], c2_ss.at[k], c2_rs.at[k], "att", xpeer)

    def hp_copy(k, block):
        return remote(hb.at[k, block], hb.at[k, block], hp_ss.at[k], hp_rs.at[k], "att", partner)

    def hx_copy(k, block):
        return remote(hb.at[k, block], hb.at[k, block], hx_ss.at[k], hx_rs.at[k], "att", xpeer)

    def hf_copy(k, block):
        return remote(hb.at[k, block], hb.at[k, block], hf_ss.at[k], hf_rs.at[k], "att", partner)

    def d_copy(k, d):
        peer = (z + d) % Z
        return remote(pd.at[k, peer], rd.at[k, d - 1], d_ss.at[k, d - 1], d_rs.at[k, d - 1], "ffn", peer)

    def block_of(ref, owner):
        return ref.at[pl.ds(owner * S, S)]

    for i, (mine, everyone) in enumerate(((q, gq), (kv, gkv))):
        remote(mine, block_of(everyone, a), qx_ss.at[i], qx_rs.at[i], "att", xpeer).start()
        remote(mine, block_of(everyone, a), qp_ss.at[i], qp_rs.at[i], "att", partner).start()
        everyone[pl.ds(a * S, S)] = mine[...]

    def qf_copy(i, everyone):
        block = block_of(everyone, xpeer)
        return remote(block, block, qf_ss.at[i], qf_rs.at[i], "att", partner)

    R = slots_row.shape[1]

    shift = S.bit_length() - 1
    spread_row = lax.broadcasted_iota(jnp.int32, (R, R * STEPS), 0) * STEPS
    spread_col = lax.broadcasted_iota(jnp.int32, (R, R * STEPS), 1)
    spread = (spread_col >= spread_row) & (spread_col < spread_row + STEPS)
    slot_at = jnp.dot(
        jnp.broadcast_to(slots_row[...].astype(f32), (8, R)).astype(bf),
        jnp.where(spread, 1.0, 0.0).astype(bf),
        preferred_element_type=f32,
    )[:1]
    row = lax.broadcasted_iota(jnp.int32, (R * STEPS, R * STEPS), 0)
    col = lax.broadcasted_iota(jnp.int32, (R * STEPS, R * STEPS), 1)
    row_slot = ((row >> (shift + 1)) << shift) + (row & (S - 1))
    row_step = (row >> shift) & (STEPS - 1)
    chosen = (row_slot.astype(f32) == slot_at) & (row_step == (col & (STEPS - 1)))
    place[...] = jnp.where(chosen, 1.0, 0.0).astype(bf)

    far = 2 * (1 - x) + (1 - c)
    for i, (mine, everyone) in enumerate(((q, gq), (kv, gkv))):
        remote(mine, block_of(everyone, xpeer), qx_ss.at[i], qx_rs.at[i], "att", xpeer).wait_recv()
        qf_copy(i, everyone).start()
    for i, (mine, everyone) in enumerate(((q, gq), (kv, gkv))):
        remote(mine, block_of(everyone, partner), qp_ss.at[i], qp_rs.at[i], "att", partner).wait_recv()
        block = block_of(everyone, far)
        remote(block, block, qf_ss.at[i], qf_rs.at[i], "att", partner).wait_recv()

    def attend(i, g):
        holder, length = holders[i], lengths[i]
        rows = gq[holder][g * QR:(g + 1) * QR]
        fresh = gkv[holder].astype(f32)
        kept = kept_rows(i)
        keys = wd_v[i // per, kept, g * 2 * HD:(g * 2 + 1) * HD]
        values = wd_v[i // per, kept, (g * 2 + 1) * HD:(g * 2 + 2) * HD]
        scale = HD ** (-0.5)
        scores = lax.dot_general(
            rows, keys, (((1,), (1,)), ((), ())), preferred_element_type=f32
        ) * scale
        column = lax.broadcasted_iota(jnp.int32, scores.shape, 1)
        scores = jnp.where(column < length, scores, -jnp.inf)
        wide = rows.astype(f32)
        step = lax.broadcasted_iota(jnp.int32, (QR, 1), 0) // groups
        new_scores = []
        for t in range(STEPS):
            at = g * 2 * STEPS + t
            score = jnp.sum(wide * fresh[at:at + 1], -1, keepdims=True) * scale
            new_scores.append(jnp.where(step >= t, score, -jnp.inf))
        top = jnp.max(scores, -1, keepdims=True)
        for score in new_scores:
            top = jnp.maximum(top, score)
        weights = jnp.exp(scores - top)
        total = jnp.sum(weights, -1, keepdims=True)
        new_weights = [jnp.exp(score - top) for score in new_scores]
        for weight in new_weights:
            total = total + weight
        mixed = jnp.dot((weights / total).astype(bf), values, preferred_element_type=f32)
        for t in range(STEPS):
            at = g * 2 * STEPS + STEPS + t
            mixed = mixed + (new_weights[t] / total).astype(bf).astype(f32) * fresh[at:at + 1]
        of[pl.ds(pl.multiple_of(i * QR, QR), QR), :] = mixed

    def t_copy(k, ss_, rs_, block, peer):
        return remote(tb.at[k, block], tb.at[k, block], ss_.at[k], rs_.at[k], "att", peer)

    heads = T // HD
    chunks = groups // heads
    for g in range(kv_local):
        @pl.loop(0, S // 8)
        def _(j):
            for n in range(8):
                if g == 0:
                    cache_copy(j * 8 + n).wait()
            for n in range(8):
                attend(j * 8 + n, g)

        for k in range(chunks):
            for t in range(STEPS):
                for n in range(heads):
                    row = t * groups + k * heads + n
                    tb[g * chunks + k, a, t * S:(t + 1) * S, n * HD:(n + 1) * HD] = of[
                        pl.ds(row, S, stride=QR), :
                    ].astype(bf)
            t_copy(g * chunks + k, tx_ss, tx_rs, a, xpeer).start()
            t_copy(g * chunks + k, tp_ss, tp_rs, a, partner).start()

    for k in range(NA):
        wcopy(wd, wd_v, wd_s, k).start()
    for k in range(NA):
        t_copy(k, tx_ss, tx_rs, xpeer, xpeer).wait_recv()
        t_copy(k, tf_ss, tf_rs, xpeer, partner).start()
    for k in range(NA):
        t_copy(k, tp_ss, tp_rs, partner, partner).wait_recv()
        t_copy(k, tf_ss, tf_rs, far, partner).wait_recv()
        attended[:, k * T:(k + 1) * T] = lax.dot_general(
            place[...], tb[k].reshape(Z * RB, T), (((0,), (0,)), ((), ())),
            preferred_element_type=f32,
        ).astype(bf)

    in_copy.wait()

    def own_half(k):
        m_copy(k).wait_recv()
        kept = kept_in[:, :, k * T:(k + 1) * T].astype(f32).reshape(2, RB, T)
        res[k, half] = (kept + om[k] + rm[k].astype(f32)).astype(bf)
        g_copy(k, half).start()
        n_copy(k, half, outer).start()

    def pass_on(k):
        g_copy(k, 1 - half).wait_recv()
        f_copy(k, 1 - half, outer).start()

    for k in range(NA):
        wcopy(wo, wo_v, wo_s, k).wait()
        fa[...] = jnp.dot(attended[...], wo_v[k], preferred_element_type=f32).reshape(fa.shape)

        @pl.when(inside == 0)
        def _():
            pa[k] = fa[...].astype(bf)
            a_copy(k, inner).start()

        @pl.when(inside > 0)
        def _():
            a_copy(k, outer).wait_recv()
            theirs = 1 - half
            sm[k] = (fa[theirs] + ra[k, theirs].astype(f32)).astype(bf)
            m_copy(k).start()
            om[k] = fa[half] + ra[k, half].astype(f32)
            if k > 0:
                own_half(k - 1)
            if k > 1:
                pass_on(k - 2)

    @pl.when(inside > 0)
    def _():
        own_half(NA - 1)
        for k in range(max(NA - 2, 0), NA):
            pass_on(k)

    squares = jnp.zeros((Z, RB, 1), f32)
    for k in range(NA):
        @pl.when(inside == 0)
        def _():
            n_copy(k, half, inner).wait_recv()
            f_copy(k, 1 - half, inner).wait_recv()

        wide = res[k].astype(f32).reshape(Z, RB, T)
        squares = squares + jnp.sum(wide * wide, -1, keepdims=True)
        h[:, k * T:(k + 1) * T] = (
            (wide * gain[:, k * T:(k + 1) * T]).astype(bf).reshape(Z * RB, T)
        )
    ss[...] = jnp.broadcast_to(squares.reshape(A, ss.shape[1], 1), ss.shape)
    for d in range(1, A):
        q_copy(d).start()

    def first(k):
        wcopy(wg, wg_v, wg_s, k).wait()
        wcopy(wu, wu_v, wu_s, k).wait()
        for i, w in enumerate((wg_v, wu_v)):
            p = jnp.dot(h[...], w[k], preferred_element_type=f32)
            fg[i] = p.reshape(fg.shape[1:])
            for xx in range(2):
                s1[k, i, xx] = fg[i, 2 * xx + (1 - c)].astype(bf)
                o1[k % 2, i, xx] = fg[i, 2 * xx + c]
        c1_copy(k).start()

    def second(k):
        c1_copy(k).wait_recv()
        for i in range(2):
            s2[k, i] = (o1[k % 2, i, 1 - x] + r1[k, i, 1 - x].astype(f32)).astype(bf)
            o2[k, i] = o1[k % 2, i, x] + r1[k, i, x].astype(f32)
        c2_copy(k).start()

    first(0)

    @pl.loop(1, NF)
    def _(k):
        first(k)
        second(k - 1)

    second(NF - 1)

    total_squares = ss[a]
    for d in range(1, A):
        q_copy(d).wait_recv()
        total_squares = total_squares + ssr[d - 1]
    inverse = lax.rsqrt(total_squares / D + epsilon)[:, :1]

    @pl.loop(0, NF)
    def _(k):
        c2_copy(k).wait_recv()
        gate = (o2[k, 0] + r2[k, 0].astype(f32)) * inverse
        up = (o2[k, 1] + r2[k, 1].astype(f32)) * inverse
        hb[k, a] = (gate / (1.0 + jnp.exp(-gate)) * up).astype(bf)
        hx_copy(k, a).start()
        hp_copy(k, a).start()

    @pl.loop(0, NF)
    def _(k):
        hx_copy(k, xpeer).wait_recv()
        hf_copy(k, xpeer).start()

    @pl.loop(0, NF)
    def _(k):
        hp_copy(k, partner).wait_recv()
        hf_copy(k, 2 * (1 - x) + (1 - c)).wait_recv()

    @pl.loop(0, NA)
    def _(n):
        wcopy(wd, wd_v, wd_s, n).wait()
        p = jnp.zeros((Z * RB, T), f32)
        for k in range(NF):
            p = p + jnp.dot(
                hb[k].reshape(Z * RB, T), wd_v[n, k * T:(k + 1) * T, :], preferred_element_type=f32
            )
        p = p.reshape(Z, RB, T)
        fa[...] = p.reshape(fa.shape)
        pd[n] = p.astype(bf)
        od[n] = fa[half, z % 2]
        for d in range(1, Z):
            d_copy(n, d).start()

    for n in range(NA):
        total = res[n, half, z % 2].astype(f32) + od[n]
        for d in range(1, Z):
            d_copy(n, d).wait_recv()
            total = total + rd[n, d - 1].astype(f32)
        out[:, :, n * T:(n + 1) * T] = total.reshape(out.shape[0], STEPS, T).astype(bf)

    for k in range(NA):
        for d in range(1, Z):
            d_copy(k, d).wait_send()

    @pl.when(inside == 0)
    def _():
        for k in range(NA):
            a_copy(k, inner).wait_send()

    @pl.when(inside > 0)
    def _():
        for k in range(NA):
            m_copy(k).wait_send()
            g_copy(k, half).wait_send()
            n_copy(k, half, outer).wait_send()
            f_copy(k, 1 - half, outer).wait_send()

    for d in range(1, A):
        q_copy(d).wait_send()
    for i, (mine, everyone) in enumerate(((q, gq), (kv, gkv))):
        remote(mine, block_of(everyone, a), qx_ss.at[i], qx_rs.at[i], "att", xpeer).wait_send()
        remote(mine, block_of(everyone, a), qp_ss.at[i], qp_rs.at[i], "att", partner).wait_send()
        qf_copy(i, everyone).wait_send()
    for k in range(NA):
        t_copy(k, tx_ss, tx_rs, a, xpeer).wait_send()
        t_copy(k, tp_ss, tp_rs, a, partner).wait_send()
        t_copy(k, tf_ss, tf_rs, xpeer, partner).wait_send()
    for k in range(NF):
        c1_copy(k).wait_send()
        c2_copy(k).wait_send()
        hp_copy(k, a).wait_send()
        hx_copy(k, a).wait_send()
        hf_copy(k, xpeer).wait_send()


def fused(holders, slots, lengths, q, kv, incoming, gain, cache, w_out, w_gate, w_up, w_down):
    Z = lax.axis_size("ffn")
    rows, kdim = slots.shape[0] * STEPS, w_out.shape[0]
    width = w_out.shape[1]
    units = w_gate.shape[1]
    RB, T = rows // Z, TILE
    NA, NF = width // T, units // T
    AB = rows // 4
    S = cache.shape[0]
    bf, f32 = jnp.bfloat16, jnp.float32
    V = pltpu.VMEM
    dma = pltpu.SemaphoreType.DMA
    vm = pl.BlockSpec(memory_space=pltpu.VMEM)
    sm = pl.BlockSpec(memory_space=pltpu.SMEM)
    hbm = pl.BlockSpec(memory_space=pl.ANY)
    scratch = [
        V((rows, rows), bf), V((incoming.shape[0] // 2,) + incoming.shape[1:], bf),
        V((4 * S,) + q.shape[1:], bf), V((4 * S,) + kv.shape[1:], bf),
        V((S * STEPS * (H // KVH), HD), f32), V((kdim // T, 4, AB, T), bf), V((rows, kdim), bf),
        V((NA, kdim, T), bf), V((NF, width, T), bf), V((NF, width, T), bf), V((NA, units, T), bf),
        V((2, 2, RB, T), f32), V((NA, 2, 2, RB, T), bf), V((NA, 2, 2, RB, T), bf), V((NA, 2, RB, T), bf),
        V((NA, 2, RB, T), bf), V((NA, 2, RB, T), f32),
        V((NA, 2, 2, RB, T), bf), V((rows, width), bf), V((4, AB, 128), f32), V((3, AB, 128), f32),
        V((2, 4, AB, T), f32), V((NF, 2, 2, AB, T), bf), V((2, 2, 2, AB, T), f32),
        V((NF, 2, 2, AB, T), bf), V((NF, 2, AB, T), bf), V((NF, 2, AB, T), f32),
        V((NF, 2, AB, T), bf), V((NF, 4, AB, T), bf),
        V((NA, Z, RB, T), bf), V((NA, RB, T), f32), V((NA, Z - 1, RB, T), bf),
        dma((NA,)), dma((NF,)), dma((NF,)), dma((NA,)),
        dma((1,)),
    ] + [dma((NA,)) for _ in range(10)] + [dma((3,)), dma((3,))]
    scratch += [dma((NF,)) for _ in range(10)] + [dma((NA, Z - 1)), dma((NA, Z - 1))]
    scratch += [dma((S,))] + [dma((2,)) for _ in range(6)] + [dma((NA,)) for _ in range(6)]
    return pl.pallas_call(
        functools.partial(layer_kernel, (Z, RB, T, NA, NF)),
        out_shape=jax.ShapeDtypeStruct((RB // STEPS, STEPS, width), bf),
        in_specs=[sm, vm, sm, vm, vm, hbm, vm, hbm, hbm, hbm, hbm, hbm],
        out_specs=vm,
        scratch_shapes=scratch,
        compiler_params=pltpu.CompilerParams(
            collective_id=1, has_side_effects=True, vmem_limit_bytes=67043328
        ),
    )(holders, slots[None], lengths, q, kv, incoming, gain, cache, w_out, w_gate, w_up, w_down)


def fits(queries, cache, w_out, w_gate, slot_of):
    slots = cache.shape[0]
    chunks = w_out.shape[1] // TILE
    return (
        lax.axis_size("att") == 4
        and lax.axis_size("ffn") == 4
        and slots % 16 == 0
        and slots & (slots - 1) == 0
        and slot_of.shape[0] == 4 * slots
        and slot_of.shape[0] * STEPS <= 128
        and cache.shape[2] == TILE
        and w_out.shape == (chunks * TILE, chunks * TILE)
        and w_gate.shape[1] % TILE == 0
        and chunks * (w_gate.shape[1] // CAP) >= slots
    )


def local_fused(
    incoming, queries, new_kv, cache, lengths, slot_of, w_out, norm_gain, w_gate, w_up, w_down
):
    slots = cache.shape[0]
    kv_local, groups = cache.shape[2] // (2 * HD), H // KVH
    q = queries.reshape(slots, STEPS, kv_local, groups, HD).transpose(0, 2, 1, 3, 4)
    kv = new_kv.reshape(slots, STEPS, kv_local, 2, HD).transpose(0, 2, 3, 1, 4)
    requests = jnp.arange(slot_of.shape[0], dtype=jnp.int32)
    own_slots = lax.axis_index("att") * slots + jnp.arange(slots, dtype=jnp.int32)
    held = slot_of[None, :] == own_slots[:, None]
    return fused(
        jnp.sum(jnp.where(held, requests[None, :], 0), 1),
        slot_of,
        lengths,
        q.reshape(slots, -1, HD),
        kv.reshape(slots, -1, HD),
        incoming,
        norm_gain[None],
        cache,
        w_out,
        w_gate,
        w_up,
        w_down,
    )


def local(
    incoming, queries, new_kv, cache, lengths, slot_of, w_out, norm_gain, w_gate, w_up, w_down
):
    if fits(queries, cache, w_out, w_gate, slot_of):
        return local_fused(
            incoming, queries, new_kv, cache, lengths, slot_of,
            w_out, norm_gain, w_gate, w_up, w_down,
        )
    ffn_count = lax.axis_size("ffn")
    att_index = lax.axis_index("att")
    ffn_index = lax.axis_index("ffn")
    request_count = slot_of.shape[0]
    slot_count = cache.shape[0]
    kv_local = cache.shape[2] // (2 * HD)
    groups = H // KVH
    score_scale = HD ** (-0.5)
    gathered_q, gathered_kv = (
        lax.all_gather(queries, "att", axis=0, tiled=True),
        lax.all_gather(new_kv, "att", axis=0, tiled=True),
    )
    holders = (
        jnp.zeros((request_count,), jnp.int32)
        .at[slot_of]
        .set(jnp.arange(request_count, dtype=jnp.int32))
    )
    my_requests = lax.dynamic_slice_in_dim(holders, att_index * slot_count, slot_count)
    query_mine = jnp.take(gathered_q, my_requests, axis=0).reshape(
        slot_count, STEPS, kv_local, groups, HD
    )
    fresh_mine = jnp.take(gathered_kv, my_requests, axis=0).reshape(
        slot_count, STEPS, kv_local, 2, HD
    )
    cache_view = cache.reshape(slot_count, CAP, kv_local, 2, HD)
    fresh_scores = (
        jnp.einsum(
            "rskgd,rtkd->rskgt",
            query_mine,
            fresh_mine[:, :, :, 0],
            preferred_element_type=jnp.float32,
        )
        * score_scale
    )
    causal = jnp.arange(STEPS)[None, :] <= jnp.arange(STEPS)[:, None]
    fresh_scores = jnp.where(causal[None, :, None, None, :], fresh_scores, -jnp.inf)
    kept_scores = (
        jnp.einsum(
            "rskgd,rckd->rskgc",
            query_mine,
            cache_view[:, :, :, 0],
            preferred_element_type=jnp.float32,
        )
        * score_scale
    )
    in_range = jnp.arange(CAP)[None, :] < lengths[:, None]
    kept_scores = jnp.where(in_range[:, None, None, None, :], kept_scores, -jnp.inf)
    top_score = jnp.maximum(jnp.max(kept_scores, -1), jnp.max(fresh_scores, -1))
    kept_exp = jnp.exp(kept_scores - top_score[..., None])
    fresh_exp = jnp.exp(fresh_scores - top_score[..., None])
    denominator = jnp.sum(kept_exp, -1) + jnp.sum(fresh_exp, -1)
    kept_prob = (kept_exp / denominator[..., None]).astype(jnp.bfloat16)
    fresh_prob = (fresh_exp / denominator[..., None]).astype(jnp.bfloat16)
    mixture = jnp.einsum(
        "rskgc,rckd->rskgd", kept_prob, cache_view[:, :, :, 1], preferred_element_type=jnp.float32
    )
    mixture = mixture + jnp.einsum(
        "rskgt,rtkd->rskgd", fresh_prob, fresh_mine[:, :, :, 1], preferred_element_type=jnp.float32
    )
    attended = mixture.astype(jnp.bfloat16).reshape(slot_count, STEPS, kv_local * groups * HD)
    shard_rows = lax.all_gather(attended, "att", axis=0, tiled=True)
    row_count = shard_rows.shape[0]
    flattened = shard_rows.reshape(row_count * STEPS, shard_rows.shape[2])
    heads_slots = jnp.dot(flattened, w_out, preferred_element_type=jnp.float32).reshape(
        row_count, STEPS, w_out.shape[1]
    )
    heads_requests = jnp.take(heads_slots, slot_of, axis=0)
    heads_total = lax.psum(heads_requests, "ffn")
    residual = (incoming.astype(jnp.float32) + heads_total).astype(jnp.bfloat16)
    residual_wide = residual.astype(jnp.float32)
    squares = lax.psum(jnp.sum(residual_wide * residual_wide, -1), "att")
    normed = (residual_wide * lax.rsqrt(squares / D + epsilon)[..., None] * norm_gain).astype(
        jnp.bfloat16
    )
    normed = normed.reshape(request_count * STEPS, normed.shape[2])
    gate_term = jnp.dot(normed, w_gate, preferred_element_type=jnp.float32)
    upward_term = jnp.dot(normed, w_up, preferred_element_type=jnp.float32)
    unit_share = lax.psum_scatter(
        jnp.concatenate([gate_term, upward_term], 1), "att", scatter_dimension=0, tiled=True
    )
    unit_width = w_gate.shape[1]
    hidden_share = (jax.nn.silu(unit_share[:, :unit_width]) * unit_share[:, unit_width:]).astype(
        jnp.bfloat16
    )
    down_part = jnp.dot(
        lax.all_gather(hidden_share, "att", axis=0, tiled=True),
        w_down,
        preferred_element_type=jnp.float32,
    )
    out_share = lax.psum_scatter(down_part, "ffn", scatter_dimension=0, tiled=True)
    row_share = request_count // ffn_count
    own_state = lax.dynamic_slice_in_dim(residual_wide, ffn_index * row_share, row_share, 0)
    return (own_state + out_share.reshape(row_share, STEPS, out_share.shape[1])).astype(
        jnp.bfloat16
    )


def solution(mesh):
    return jax.shard_map(
        local,
        mesh=mesh,
        in_specs=(
            P("parts", None, "att"),
            P(("parts", "att"), None, "ffn"),
            P(("parts", "att"), None, "ffn"),
            P(("parts", "att"), None, "ffn"),
            P(("parts", "att")),
            P("parts"),
            P("ffn", "att"),
            P("att"),
            P("att", "ffn"),
            P("att", "ffn"),
            P("ffn", "att"),
        ),
        out_specs=P(("parts", "ffn"), None, "att"),
        check_vma=False,
    )
```

profile of v0, /device:TPU:0, one launch (start us, length us, event | category | flops | bytes accessed | tf_op | source)
XLA Modules:
  0.0 91.3 jit_solution(12362239469077496201)
XLA Ops:
  0.0 1.3 %select_reduce_fusion.holders = s32[16]{0:T(128)} fusion(s32[64]{0:T(128)} %param.16, s32[16]{0:T(128)S(1)} %iota_add_fusion), kind=kLoop, calls=%fused_computation | loop fusion | flops 3056 | bytes 384 | tf_op jit(solution)/shard_map/reduce_sum | solution.py:487
  1.3 1.0 %reshape.17 = bf16[16,2,2,8,128]{4,3,2,1,0:T(8,128)(2,1)S(1)} reshape(bf16[16,2,2048]{2,1,0:T(2,128)(2,1)} %param.12) | data formatting | bytes 262144 | tf_op jit(solution)/shard_map/reshape | solution.py:481
  2.3 0.7 copy.14
  3.0 86.6 %shard_map.109 = bf16[16,2,2048]{2,1,0:T(2,128)(2,1)} custom-call(s32[16]{0:T(128)} %select_reduce_fusion.holders, s32[1,64]{1,0:T(1,128)} %bitcast.13, s32[16]{0:T(128)} %lengths.1, bf16[16,32,128]{2,1,0:T(8,128)(2,1)} %bitcast.10, bf16[16,8,128]{2,1,0:T(8,128)(2,1)} %bitcast.11, bf16[64,2,2048]{2,1,0:T(2,128)(2,1)} %incoming.1, f32[1,2048]{1,0:T(1,128)} %bitcast.12, ...), custom_call_target="tpu_custom_call" | custom-call | tf_op jit(solution)/shard_map/pallas_call | solution.py:447
  89.6 1.7 %copy.17 = bf16[16,2,2048]{2,1,0:T(2,128)(2,1)} copy(bf16[16,2,2048]{2,1,0:T(2,128)(2,1)} %shard_map.109) | data formatting | bytes 262144
  (1 shorter events, 0.0 us)
where the time goes:
time: 91.5 us; the launch traced here: 91.3 us
  Pallas kernels  86.6 us (95%)
  local copies, waits for them, and re-layouts  3.32 us (4%)
  other arithmetic  1.34 us (1%)
    pallas_call x1, Pallas kernels, fused(): pl.pallas_call(functools.partial(layer_kernel, (Z, RB, T, NA, NF)), out_s...  86.6 us

commit v1 on v0

--- a/solution.py
+++ b/solution.py
@@ -24,18 +24,18 @@
     cfg, holders, slots_row, lengths, q, kv, incoming, gain, cache, wo, wg, wu, wd, out,
     place, kept_in, gq, gkv, of, tb, attended,
     wo_v, wg_v, wu_v, wd_v,
-    fa, pa, ra, sm, rm, om, res, h, ss, ssr,
+    pa, ra, rm, res, h, ss, ssr,
     fg, s1, o1, r1, s2, o2, r2, hb,
     pd, od, rd,
     wo_s, wg_s, wu_s, wd_s,
-    in_s, a_ss, a_rs, m_ss, m_rs, g_ss, g_rs, n_ss, n_rs, f_ss, f_rs, q_ss, q_rs,
+    in_s, a_ss, a_rs, m_ss, m_rs, n_ss, n_rs, q_ss, q_rs,
     c1_ss, c1_rs, c2_ss, c2_rs,
     hp_ss, hp_rs, hx_ss, hx_rs, hf_ss, hf_rs,
     d_ss, d_rs,
     cache_s, qp_ss, qp_rs, qx_ss, qx_rs, qf_ss, qf_rs,
     tp_ss, tp_rs, tx_ss, tx_rs, tf_ss, tf_rs,
 ):
-    Z, RB, T, NA, NF = cfg
+    Z, HR, BR, T, NA, NF = cfg
     S = cache.shape[0]
     kv_local = cache.shape[2] // (2 * HD)
     groups = H // KVH
@@ -47,6 +47,7 @@
     x, c = a // 2, a % 2
     partner = 2 * x + (1 - c)
     xpeer = 2 * (1 - x) + c
+    far = 2 * (1 - x) + (1 - c)
     bf, f32 = jnp.bfloat16, jnp.float32
 
     def wcopy(src, dst, sem, k):
@@ -64,10 +65,7 @@
     def _(i):
         cache_copy(i).start()
 
-    half = z // 2
-    in_copy = pltpu.make_async_copy(
-        incoming.at[pl.ds(half * kept_in.shape[0], kept_in.shape[0])], kept_in, in_s.at[0]
-    )
+    in_copy = pltpu.make_async_copy(incoming, kept_in, in_s.at[0])
     in_copy.start()
     for k in range(NA):
         wcopy(wo, wo_v, wo_s, k).start()
@@ -88,54 +86,51 @@
             device_id={axis: peer}, device_id_type=MESH,
         )
 
+    half = z // 2
     inside = z * (Z - 1 - z)
     inner = 1 + half
     outer = 3 * (z - 1)
     other = 3 - z
 
-    def half_of(ref, k, which):
-        return ref.at[k, which]
-
-    def a_copy(k, peer):
-        return remote(pa.at[k], ra.at[k], a_ss.at[k], a_rs.at[k], "ffn", peer)
-
-    def m_copy(k):
-        return remote(sm.at[k], rm.at[k], m_ss.at[k], m_rs.at[k], "ffn", other)
-
-    def g_copy(k, which):
-        block = half_of(res, k, which)
-        return remote(block, block, g_ss.at[k], g_rs.at[k], "ffn", other)
-
-    def n_copy(k, which, peer):
-        block = half_of(res, k, which)
-        return remote(block, block, n_ss.at[k], n_rs.at[k], "ffn", peer)
-
-    def f_copy(k, which, peer):
-        block = half_of(res, k, which)
-        return remote(block, block, f_ss.at[k], f_rs.at[k], "ffn", peer)
-
-    def q_copy(d):
+    def a_copy(j, peer):
+        return remote(pa.at[j], ra.at[j], a_ss.at[j], a_rs.at[j], "ffn", peer)
+
+    def m_copy(j):
+        return remote(pa.at[j], rm.at[j], m_ss.at[j], m_rs.at[j], "ffn", other)
+
+    def n_copy(j, peer):
+        return remote(res.at[j], res.at[j], n_ss.at[j], n_rs.at[j], "ffn", peer)
+
+    def q_copy(hh, d):
         peer = (a + d) % A
-        return remote(ss.at[peer], ssr.at[d - 1], q_ss.at[d - 1], q_rs.at[d - 1], "att", peer)
-
-    def c1_copy(k):
-        return remote(s1.at[k], r1.at[k], c1_ss.at[k], c1_rs.at[k], "att", partner)
-
-    def c2_copy(k):
-        return remote(s2.at[k], r2.at[k], c2_ss.at[k], c2_rs.at[k], "att", xpeer)
-
-    def hp_copy(k, block):
-        return remote(hb.at[k, block], hb.at[k, block], hp_ss.at[k], hp_rs.at[k], "att", partner)
-
-    def hx_copy(k, block):
-        return remote(hb.at[k, block], hb.at[k, block], hx_ss.at[k], hx_rs.at[k], "att", xpeer)
-
-    def hf_copy(k, block):
-        return remote(hb.at[k, block], hb.at[k, block], hf_ss.at[k], hf_rs.at[k], "att", partner)
-
-    def d_copy(k, d):
+        at = hh * (A - 1) + d - 1
+        return remote(ss.at[hh, peer], ssr.at[hh, d - 1], q_ss.at[at], q_rs.at[at], "att", peer)
+
+    def c1_copy(hh, k):
+        j = hh * NF + k
+        return remote(s1.at[j], r1.at[j], c1_ss.at[j], c1_rs.at[j], "att", partner)
+
+    def c2_copy(hh, k):
+        j = hh * NF + k
+        return remote(s2.at[j], r2.at[j], c2_ss.at[j], c2_rs.at[j], "att", xpeer)
+
+    def h_copy(ss_, rs_, hh, k, block, peer):
+        j = hh * NF + k
+        return remote(hb.at[j, block], hb.at[j, block], ss_.at[j], rs_.at[j], "att", peer)
+
+    def hp_copy(hh, k, block):
+        return h_copy(hp_ss, hp_rs, hh, k, block, partner)
+
+    def hx_copy(hh, k, block):
+        return h_copy(hx_ss, hx_rs, hh, k, block, xpeer)
+
+    def hf_copy(hh, k, block):
+        return h_copy(hf_ss, hf_rs, hh, k, block, partner)
+
+    def d_copy(hh, n, d):
         peer = (z + d) % Z
-        return remote(pd.at[k, peer], rd.at[k, d - 1], d_ss.at[k, d - 1], d_rs.at[k, d - 1], "ffn", peer)
+        j = hh * NA + n
+        return remote(pd.at[j, peer], rd.at[j, d - 1], d_ss.at[j, d - 1], d_rs.at[j, d - 1], "ffn", peer)
 
     def block_of(ref, owner):
         return ref.at[pl.ds(owner * S, S)]
@@ -150,14 +145,20 @@
         return remote(block, block, qf_ss.at[i], qf_rs.at[i], "att", partner)
 
     R = slots_row.shape[1]
-
     shift = S.bit_length() - 1
-    spread_row = lax.broadcasted_iota(jnp.int32, (R, R * STEPS), 0) * STEPS
-    spread_col = lax.broadcasted_iota(jnp.int32, (R, R * STEPS), 1)
-    spread = (spread_col >= spread_row) & (spread_col < spread_row + STEPS)
+    cut = HR.bit_length() - 1
+    deep = BR.bit_length() - 1
+    owned = R // Z
+
+    def request_of(rows):
+        piece, owner, own = rows >> cut, (rows >> deep) & (Z - 1), (rows & (BR - 1)) >> 1
+        return owner * owned + piece * (BR // STEPS) + own
+
+    spread_row = lax.broadcasted_iota(jnp.int32, (R, R * STEPS), 0)
+    spread_col = request_of(lax.broadcasted_iota(jnp.int32, (R, R * STEPS), 1))
     slot_at = jnp.dot(
         jnp.broadcast_to(slots_row[...].astype(f32), (8, R)).astype(bf),
-        jnp.where(spread, 1.0, 0.0).astype(bf),
+        jnp.where(spread_col == spread_row, 1.0, 0.0).astype(bf),
         preferred_element_type=f32,
     )[:1]
     row = lax.broadcasted_iota(jnp.int32, (R * STEPS, R * STEPS), 0)
@@ -167,7 +168,6 @@
     chosen = (row_slot.astype(f32) == slot_at) & (row_step == (col & (STEPS - 1)))
     place[...] = jnp.where(chosen, 1.0, 0.0).astype(bf)
 
-    far = 2 * (1 - x) + (1 - c)
     for i, (mine, everyone) in enumerate(((q, gq), (kv, gkv))):
         remote(mine, block_of(everyone, xpeer), qx_ss.at[i], qx_rs.at[i], "att", xpeer).wait_recv()
         qf_copy(i, everyone).start()
@@ -239,163 +239,243 @@
     for k in range(NA):
         t_copy(k, tx_ss, tx_rs, xpeer, xpeer).wait_recv()
         t_copy(k, tf_ss, tf_rs, xpeer, partner).start()
+    in_copy.wait()
+
+    @pl.when(inside > 0)
+    def _():
+        for j in range(2 * NA):
+            hh, k = j // NA, j % NA
+            for owner in range(Z):
+                at = owner * owned + hh * (BR // STEPS)
+                block = kept_in[at:at + BR // STEPS, :, k * T:(k + 1) * T]
+                res[j, owner * BR:(owner + 1) * BR, :] = block.reshape(BR, T)
+
     for k in range(NA):
         t_copy(k, tp_ss, tp_rs, partner, partner).wait_recv()
         t_copy(k, tf_ss, tf_rs, far, partner).wait_recv()
         attended[:, k * T:(k + 1) * T] = lax.dot_general(
-            place[...], tb[k].reshape(Z * RB, T), (((0,), (0,)), ((), ())),
+            place[...], tb[k].reshape(2 * HR, T), (((0,), (0,)), ((), ())),
             preferred_element_type=f32,
         ).astype(bf)
 
-    in_copy.wait()
-
-    def own_half(k):
-        m_copy(k).wait_recv()
-        kept = kept_in[:, :, k * T:(k + 1) * T].astype(f32).reshape(2, RB, T)
-        res[k, half] = (kept + om[k] + rm[k].astype(f32)).astype(bf)
-        g_copy(k, half).start()
-        n_copy(k, half, outer).start()
-
-    def pass_on(k):
-        g_copy(k, 1 - half).wait_recv()
-        f_copy(k, 1 - half, outer).start()
-
-    for k in range(NA):
-        wcopy(wo, wo_v, wo_s, k).wait()
-        fa[...] = jnp.dot(attended[...], wo_v[k], preferred_element_type=f32).reshape(fa.shape)
-
-        @pl.when(inside == 0)
-        def _():
-            pa[k] = fa[...].astype(bf)
-            a_copy(k, inner).start()
-
-        @pl.when(inside > 0)
-        def _():
-            a_copy(k, outer).wait_recv()
-            theirs = 1 - half
-            sm[k] = (fa[theirs] + ra[k, theirs].astype(f32)).astype(bf)
-            m_copy(k).start()
-            om[k] = fa[half] + ra[k, half].astype(f32)
-            if k > 0:
-                own_half(k - 1)
-            if k > 1:
-                pass_on(k - 2)
+    def partial_sum(j):
+        hh, k = j // NA, j % NA
+        rows = attended[hh * HR:(hh + 1) * HR, :]
+        return jnp.dot(rows, wo_v[k], preferred_element_type=f32)
+
+    @pl.when(inside == 0)
+    def _():
+        for hh in range(2):
+            @pl.loop(0, NA)
+            def _(k):
+                if hh == 0:
+                    wcopy(wo, wo_v, wo_s, k).wait()
+                j = hh * NA + k
+                rows = attended[hh * HR:(hh + 1) * HR, :]
+                pa[j] = jnp.dot(rows, wo_v[k], preferred_element_type=f32).astype(bf)
+                a_copy(j, inner).start()
+
+    def add_outer(j):
+        if j < NA:
+            wcopy(wo, wo_v, wo_s, j).wait()
+        p = partial_sum(j)
+        a_copy(j, outer).wait_recv()
+        pa[j] = (p + ra[j].astype(f32)).astype(bf)
+        m_copy(j).start()
+
+    def add_other(j):
+        m_copy(j).wait_recv()
+        both = pa[j].astype(f32) + rm[j].astype(f32)
+        res[j] = (res[j].astype(f32) + both).astype(bf)
+        n_copy(j, outer).start()
+
+    ahead = 2 * NA - 2
+    lag = 2
 
     @pl.when(inside > 0)
     def _():
-        own_half(NA - 1)
-        for k in range(max(NA - 2, 0), NA):
-            pass_on(k)
-
-    squares = jnp.zeros((Z, RB, 1), f32)
-    for k in range(NA):
-        @pl.when(inside == 0)
-        def _():
-            n_copy(k, half, inner).wait_recv()
-            f_copy(k, 1 - half, inner).wait_recv()
-
-        wide = res[k].astype(f32).reshape(Z, RB, T)
-        squares = squares + jnp.sum(wide * wide, -1, keepdims=True)
-        h[:, k * T:(k + 1) * T] = (
-            (wide * gain[:, k * T:(k + 1) * T]).astype(bf).reshape(Z * RB, T)
-        )
-    ss[...] = jnp.broadcast_to(squares.reshape(A, ss.shape[1], 1), ss.shape)
-    for d in range(1, A):
-        q_copy(d).start()
-
-    def first(k):
-        wcopy(wg, wg_v, wg_s, k).wait()
-        wcopy(wu, wu_v, wu_s, k).wait()
+        for j in range(ahead):
+            add_outer(j)
+            if j >= lag:
+                add_other(j - lag)
+
+    def normed(hh):
+        squares = jnp.zeros((HR, 1), f32)
+        for k in range(NA):
+            j = hh * NA + k
+
+            @pl.when(inside == 0)
+            def _():
+                n_copy(j, inner).wait_recv()
+
+            wide = res[j].astype(f32)
+            squares = squares + jnp.sum(wide * wide, -1, keepdims=True)
+            h[hh, :, k * T:(k + 1) * T] = (wide * gain[:, k * T:(k + 1) * T]).astype(bf)
+        ss[hh] = jnp.broadcast_to(squares.reshape(A, BR, 1), ss.shape[1:])
+        for d in range(1, A):
+            q_copy(hh, d).start()
+
+    def first(hh, k):
+        if hh == 0:
+            wcopy(wg, wg_v, wg_s, k).wait()
+            wcopy(wu, wu_v, wu_s, k).wait()
         for i, w in enumerate((wg_v, wu_v)):
-            p = jnp.dot(h[...], w[k], preferred_element_type=f32)
+            p = jnp.dot(h[hh], w[k], preferred_element_type=f32)
             fg[i] = p.reshape(fg.shape[1:])
             for xx in range(2):
-                s1[k, i, xx] = fg[i, 2 * xx + (1 - c)].astype(bf)
+                s1[hh * NF + k, i, xx] = fg[i, 2 * xx + (1 - c)].astype(bf)
                 o1[k % 2, i, xx] = fg[i, 2 * xx + c]
-        c1_copy(k).start()
-
-    def second(k):
-        c1_copy(k).wait_recv()
+        c1_copy(hh, k).start()
+
+    def second(hh, k):
+        c1_copy(hh, k).wait_recv()
+        j = hh * NF + k
         for i in range(2):
-            s2[k, i] = (o1[k % 2, i, 1 - x] + r1[k, i, 1 - x].astype(f32)).astype(bf)
-            o2[k, i] = o1[k % 2, i, x] + r1[k, i, x].astype(f32)
-        c2_copy(k).start()
-
-    first(0)
-
-    @pl.loop(1, NF)
-    def _(k):
-        first(k)
-        second(k - 1)
-
-    second(NF - 1)
-
-    total_squares = ss[a]
-    for d in range(1, A):
-        q_copy(d).wait_recv()
-        total_squares = total_squares + ssr[d - 1]
-    inverse = lax.rsqrt(total_squares / D + epsilon)[:, :1]
+            s2[j, i] = (o1[k % 2, i, 1 - x] + r1[j, i, 1 - x].astype(f32)).astype(bf)
+            o2[j, i] = o1[k % 2, i, x] + r1[j, i, x].astype(f32)
+        c2_copy(hh, k).start()
+
+    def inverse_of(hh):
+        total_squares = ss[hh, a]
+        for d in range(1, A):
+            q_copy(hh, d).wait_recv()
+            total_squares = total_squares + ssr[hh, d - 1]
+        return lax.rsqrt(total_squares / D + epsilon)[:, :1]
+
+    def third(hh, k, inverse):
+        c2_copy(hh, k).wait_recv()
+        j = hh * NF + k
+        gate = (o2[j, 0] + r2[j, 0].astype(f32)) * inverse
+        up = (o2[j, 1] + r2[j, 1].astype(f32)) * inverse
+        hb[j, a] = (gate / (1.0 + jnp.exp(-gate)) * up).astype(bf)
+        hx_copy(hh, k, a).start()
+        hp_copy(hh, k, a).start()
+
+    def fourth(hh, k):
+        hx_copy(hh, k, xpeer).wait_recv()
+        hf_copy(hh, k, xpeer).start()
+
+    def fifth(hh):
+        @pl.loop(0, NF)
+        def _(k):
+            hp_copy(hh, k, partner).wait_recv()
+            hf_copy(hh, k, far).wait_recv()
+
+    def down(hh, n):
+        if hh == 0:
+            wcopy(wd, wd_v, wd_s, n).wait()
+        p = jnp.zeros((HR, T), f32)
+        for k in range(NF):
+            p = p + jnp.dot(
+                hb[hh * NF + k].reshape(HR, T), wd_v[n, k * T:(k + 1) * T, :],
+                preferred_element_type=f32,
+            )
+        p = p.reshape(Z, BR, T)
+        fg[0] = p
+        j = hh * NA + n
+        pd[j] = p.astype(bf)
+        od[j] = fg[0, z]
+        for d in range(1, Z):
+            d_copy(hh, n, d).start()
+
+    relays = {
+        1: ((add_outer, ahead), (add_other, ahead - 2)),
+        3: ((add_outer, ahead + 1), (add_other, ahead - 1)),
+        5: ((add_other, ahead),),
+        6: ((add_other, ahead + 1),),
+    }
+
+    normed(0)
 
     @pl.loop(0, NF)
     def _(k):
-        c2_copy(k).wait_recv()
-        gate = (o2[k, 0] + r2[k, 0].astype(f32)) * inverse
-        up = (o2[k, 1] + r2[k, 1].astype(f32)) * inverse
-        hb[k, a] = (gate / (1.0 + jnp.exp(-gate)) * up).astype(bf)
-        hx_copy(k, a).start()
-        hp_copy(k, a).start()
+        first(0, k)
+
+        @pl.when(k > 0)
+        def _():
+            second(0, k - 1)
+
+        for at, todo in relays.items():
+            @pl.when((inside > 0) & (k == min(at, NF - 1)))
+            def _():
+                for what, j in todo:
+                    what(j)
+
+    second(0, NF - 1)
+    normed(1)
+    inverse = inverse_of(0)
 
     @pl.loop(0, NF)
     def _(k):
-        hx_copy(k, xpeer).wait_recv()
-        hf_copy(k, xpeer).start()
+        first(1, k)
+
+        @pl.when(k > 0)
+        def _():
+            second(1, k - 1)
+
+        third(0, k, inverse)
+
+        @pl.when(k > 2)
+        def _():
+            fourth(0, k - 3)
+
+    second(1, NF - 1)
+    for k in range(max(NF - 3, 0), NF):
+        fourth(0, k)
+    inverse_b = inverse_of(1)
 
     @pl.loop(0, NF)
     def _(k):
-        hp_copy(k, partner).wait_recv()
-        hf_copy(k, 2 * (1 - x) + (1 - c)).wait_recv()
+        third(1, k, inverse_b)
+
+    fifth(0)
+    share = -(-NF // NA)
 
     @pl.loop(0, NA)
     def _(n):
-        wcopy(wd, wd_v, wd_s, n).wait()
-        p = jnp.zeros((Z * RB, T), f32)
-        for k in range(NF):
-            p = p + jnp.dot(
-                hb[k].reshape(Z * RB, T), wd_v[n, k * T:(k + 1) * T, :], preferred_element_type=f32
-            )
-        p = p.reshape(Z, RB, T)
-        fa[...] = p.reshape(fa.shape)
-        pd[n] = p.astype(bf)
-        od[n] = fa[half, z % 2]
-        for d in range(1, Z):
-            d_copy(n, d).start()
-
-    for n in range(NA):
-        total = res[n, half, z % 2].astype(f32) + od[n]
-        for d in range(1, Z):
-            d_copy(n, d).wait_recv()
-            total = total + rd[n, d - 1].astype(f32)
-        out[:, :, n * T:(n + 1) * T] = total.reshape(out.shape[0], STEPS, T).astype(bf)
-
-    for k in range(NA):
-        for d in range(1, Z):
-            d_copy(k, d).wait_send()
+        down(0, n)
+
+        @pl.loop(n * share, jnp.minimum((n + 1) * share, NF))
+        def _(k):
+            fourth(1, k)
+
+    fifth(1)
+
+    @pl.loop(0, NA)
+    def _(n):
+        down(1, n)
+
+    for hh in range(2):
+        for n in range(NA):
+            j = hh * NA + n
+            total = res[j, pl.ds(pl.multiple_of(z * BR, BR), BR), :].astype(f32) + od[j]
+            for d in range(1, Z):
+                d_copy(hh, n, d).wait_recv()
+                total = total + rd[j, d - 1].astype(f32)
+            at = hh * (BR // STEPS)
+            out[at:at + BR // STEPS, :, n * T:(n + 1) * T] = total.reshape(
+                BR // STEPS, STEPS, T
+            ).astype(bf)
+
+    for hh in range(2):
+        for n in range(NA):
+            for d in range(1, Z):
+                d_copy(hh, n, d).wait_send()
 
     @pl.when(inside == 0)
     def _():
-        for k in range(NA):
-            a_copy(k, inner).wait_send()
+        for j in range(2 * NA):
+            a_copy(j, inner).wait_send()
 
     @pl.when(inside > 0)
     def _():
-        for k in range(NA):
-            m_copy(k).wait_send()
-            g_copy(k, half).wait_send()
-            n_copy(k, half, outer).wait_send()
-            f_copy(k, 1 - half, outer).wait_send()
-
-    for d in range(1, A):
-        q_copy(d).wait_send()
+        for j in range(2 * NA):
+            m_copy(j).wait_send()
+            n_copy(j, outer).wait_send()
+
+    for hh in range(2):
+        for d in range(1, A):
+            q_copy(hh, d).wait_send()
     for i, (mine, everyone) in enumerate(((q, gq), (kv, gkv))):
         remote(mine, block_of(everyone, a), qx_ss.at[i], qx_rs.at[i], "att", xpeer).wait_send()
         remote(mine, block_of(everyone, a), qp_ss.at[i], qp_rs.at[i], "att", partner).wait_send()
@@ -404,12 +484,14 @@
         t_copy(k, tx_ss, tx_rs, a, xpeer).wait_send()
         t_copy(k, tp_ss, tp_rs, a, partner).wait_send()
         t_copy(k, tf_ss, tf_rs, xpeer, partner).wait_send()
-    for k in range(NF):
-        c1_copy(k).wait_send()
-        c2_copy(k).wait_send()
-        hp_copy(k, a).wait_send()
-        hx_copy(k, a).wait_send()
-        hf_copy(k, xpeer).wait_send()
+    for hh in range(2):
+        @pl.loop(0, NF)
+        def _(k):
+            c1_copy(hh, k).wait_send()
+            c2_copy(hh, k).wait_send()
+            hp_copy(hh, k, a).wait_send()
+            hx_copy(hh, k, a).wait_send()
+            hf_copy(hh, k, xpeer).wait_send()
 
 
 def fused(holders, slots, lengths, q, kv, incoming, gain, cache, w_out, w_gate, w_up, w_down):
@@ -417,7 +499,9 @@
     rows, kdim = slots.shape[0] * STEPS, w_out.shape[0]
     width = w_out.shape[1]
     units = w_gate.shape[1]
-    RB, T = rows // Z, TILE
+    T = TILE
+    HR = rows // 2
+    BR = HR // Z
     NA, NF = width // T, units // T
     AB = rows // 4
     S = cache.shape[0]
@@ -428,25 +512,24 @@
     sm = pl.BlockSpec(memory_space=pltpu.SMEM)
     hbm = pl.BlockSpec(memory_space=pl.ANY)
     scratch = [
-        V((rows, rows), bf), V((incoming.shape[0] // 2,) + incoming.shape[1:], bf),
+        V((rows, rows), bf), V(incoming.shape, bf),
         V((4 * S,) + q.shape[1:], bf), V((4 * S,) + kv.shape[1:], bf),
         V((S * STEPS * (H // KVH), HD), f32), V((kdim // T, 4, AB, T), bf), V((rows, kdim), bf),
         V((NA, kdim, T), bf), V((NF, width, T), bf), V((NF, width, T), bf), V((NA, units, T), bf),
-        V((2, 2, RB, T), f32), V((NA, 2, 2, RB, T), bf), V((NA, 2, 2, RB, T), bf), V((NA, 2, RB, T), bf),
-        V((NA, 2, RB, T), bf), V((NA, 2, RB, T), f32),
-        V((NA, 2, 2, RB, T), bf), V((rows, width), bf), V((4, AB, 128), f32), V((3, AB, 128), f32),
-        V((2, 4, AB, T), f32), V((NF, 2, 2, AB, T), bf), V((2, 2, 2, AB, T), f32),
-        V((NF, 2, 2, AB, T), bf), V((NF, 2, AB, T), bf), V((NF, 2, AB, T), f32),
-        V((NF, 2, AB, T), bf), V((NF, 4, AB, T), bf),
-        V((NA, Z, RB, T), bf), V((NA, RB, T), f32), V((NA, Z - 1, RB, T), bf),
+        V((2 * NA, HR, T), bf), V((2 * NA, HR, T), bf), V((2 * NA, HR, T), bf), V((2 * NA, HR, T), bf),
+        V((2, HR, width), bf), V((2, 4, BR, 128), f32), V((2, 3, BR, 128), f32),
+        V((2, 4, BR, T), f32), V((2 * NF, 2, 2, BR, T), bf), V((2, 2, 2, BR, T), f32),
+        V((2 * NF, 2, 2, BR, T), bf), V((2 * NF, 2, BR, T), bf), V((2 * NF, 2, BR, T), f32),
+        V((2 * NF, 2, BR, T), bf), V((2 * NF, 4, BR, T), bf),
+        V((2 * NA, Z, BR, T), bf), V((2 * NA, BR, T), f32), V((2 * NA, Z - 1, BR, T), bf),
         dma((NA,)), dma((NF,)), dma((NF,)), dma((NA,)),
         dma((1,)),
-    ] + [dma((NA,)) for _ in range(10)] + [dma((3,)), dma((3,))]
-    scratch += [dma((NF,)) for _ in range(10)] + [dma((NA, Z - 1)), dma((NA, Z - 1))]
+    ] + [dma((2 * NA,)) for _ in range(6)] + [dma((6,)), dma((6,))]
+    scratch += [dma((2 * NF,)) for _ in range(10)] + [dma((2 * NA, Z - 1)), dma((2 * NA, Z - 1))]
     scratch += [dma((S,))] + [dma((2,)) for _ in range(6)] + [dma((NA,)) for _ in range(6)]
     return pl.pallas_call(
-        functools.partial(layer_kernel, (Z, RB, T, NA, NF)),
-        out_shape=jax.ShapeDtypeStruct((RB // STEPS, STEPS, width), bf),
+        functools.partial(layer_kernel, (Z, HR, BR, T, NA, NF)),
+        out_shape=jax.ShapeDtypeStruct((rows // Z // STEPS, STEPS, width), bf),
         in_specs=[sm, vm, sm, vm, vm, hbm, vm, hbm, hbm, hbm, hbm, hbm],
         out_specs=vm,
         scratch_shapes=scratch,

time: 91.5 us -> 86.7 us (0.948)
  Pallas kernels: 86.6 us -> 81.9 us
    pallas_call x1, Pallas kernels: 86.6 us -> 81.9 us  [fused(): pl.pallas_call(functools.partial(layer_kernel, (Z, HR, BR, T, NA, NF)), o...]
where the time goes in v1:
time: 86.7 us; the launch traced here: 86.6 us
  Pallas kernels  81.9 us (94%)
  local copies, waits for them, and re-layouts  3.32 us (4%)
  other arithmetic  1.34 us (2%)
    pallas_call x1, Pallas kernels, fused(): pl.pallas_call(functools.partial(layer_kernel, (Z, HR, BR, T, NA, NF)), o...  81.9 us

profile of v1, /device:TPU:0, one launch (start us, length us, event | category | flops | bytes accessed | tf_op | source)
XLA Modules:
  0.0 86.6 jit_solution(5426236525908029407)
XLA Ops:
  0.0 1.3 %select_reduce_fusion.holders = s32[16]{0:T(128)} fusion(s32[64]{0:T(128)} %param.16, s32[16]{0:T(128)S(1)} %iota_add_fusion), kind=kLoop, calls=%fused_computation | loop fusion | flops 3056 | bytes 384 | tf_op jit(solution)/shard_map/reduce_sum | solution.py:570
  1.3 1.0 %reshape.17 = bf16[16,2,2,8,128]{4,3,2,1,0:T(8,128)(2,1)S(1)} reshape(bf16[16,2,2048]{2,1,0:T(2,128)(2,1)} %param.12) | data formatting | bytes 262144 | tf_op jit(solution)/shard_map/reshape | solution.py:564
  2.3 0.7 copy.14
  3.0 81.9 %shard_map.109 = bf16[16,2,2048]{2,1,0:T(2,128)(2,1)} custom-call(s32[16]{0:T(128)} %select_reduce_fusion.holders, s32[1,64]{1,0:T(1,128)} %bitcast.13, s32[16]{0:T(128)} %lengths.1, bf16[16,32,128]{2,1,0:T(8,128)(2,1)} %bitcast.10, bf16[16,8,128]{2,1,0:T(8,128)(2,1)} %bitcast.11, bf16[64,2,2048]{2,1,0:T(2,128)(2,1)} %incoming.1, f32[1,2048]{1,0:T(1,128)} %bitcast.12, ...), custom_call_target="tpu_custom_call" | custom-call | tf_op jit(solution)/shard_map/pallas_call | solution.py:530
  84.9 1.7 %copy.17 = bf16[16,2,2048]{2,1,0:T(2,128)(2,1)} copy(bf16[16,2,2048]{2,1,0:T(2,128)(2,1)} %shard_map.109) | data formatting | bytes 262144
  (1 shorter events, 0.0 us)

commit v2 on v1

v2 whole, which is shorter than its diff:
```python
import functools

import jax
import jax.numpy as jnp
from jax import lax
from jax.experimental import pallas as pl
from jax.experimental.pallas import tpu as pltpu
from jax.sharding import PartitionSpec as P

D = 8192
H = 64
KVH = 8
HD = 128
STEPS = 2
CAP = 640


epsilon = 1e-05
TILE = 512
MESH = pl.DeviceIdType.MESH


def layer_kernel(
    cfg, slots, slots_row, lengths, q, kv, incoming, gain, cache, wo, wg, wu, wd, out,
    holders, place, kept_in, gq, gkv, of, pair, tb, attended,
    wo_v, wg_v, wu_v, wd_v,
    pa, ra, rm, res, h, sq, inv, ss, ssr,
    acc, s1, r1, s2, r2, hb,
    rd,
    wo_s, wg_s, wu_s, wd_s,
    in_s, a_ss, a_rs, m_ss, m_rs, n_ss, n_rs, q_ss, q_rs,
    c1_ss, c1_rs, c2_ss, c2_rs,
    hp_ss, hp_rs, hx_ss, hx_rs, hf_ss, hf_rs,
    d_ss, d_rs,
    cache_s, qp_ss, qp_rs, qx_ss, qx_rs, qf_ss, qf_rs,
    tp_ss, tp_rs, tx_ss, tx_rs, tf_ss, tf_rs,
):
    Z, HR, BR, T, TK, NA, NT, NF = cfg
    NK = NT // 2
    S = cache.shape[0]
    kv_local = cache.shape[2] // (2 * HD)
    groups = H // KVH
    QR = STEPS * groups
    per = wd_v.shape[1] // CAP
    A = 4
    z = lax.axis_index("ffn")
    a = lax.axis_index("att")
    x, c = a // 2, a % 2
    partner = 2 * x + (1 - c)
    xpeer = 2 * (1 - x) + c
    far = 2 * (1 - x) + (1 - c)
    bf, f32 = jnp.bfloat16, jnp.float32

    def wcopy(src, dst, sem, k):
        return pltpu.make_async_copy(
            src.at[:, pl.ds(pl.multiple_of(k * T, T), T)], dst.at[k], sem.at[k]
        )

    def kept_rows(i):
        return pl.ds(pl.multiple_of((i % per) * CAP, CAP), CAP)

    def cache_copy(i):
        return pltpu.make_async_copy(cache.at[i], wd_v.at[i // per, kept_rows(i)], cache_s.at[i])

    @pl.loop(0, S)
    def _(i):
        cache_copy(i).start()

    in_copy = pltpu.make_async_copy(incoming, kept_in, in_s.at[0])
    in_copy.start()
    for k in range(NA):
        wcopy(wo, wo_v, wo_s, k).start()
    for k in range(NF):
        wcopy(wg, wg_v, wg_s, k).start()
        wcopy(wu, wu_v, wu_s, k).start()

    SG = S // 2
    for head in range(kv_local * groups):
        g, j = head // groups, head % groups
        block = q[:, :, head * HD:(head + 1) * HD].astype(f32)
        pair[...] = block.reshape(pair.shape)
        for t in range(STEPS):
            of[pl.ds(g * QR + t * groups + j, S, stride=kv_local * QR), :] = pair[
                pl.ds(t, S, stride=STEPS), :
            ]
    gq[pl.ds(a * S, S)] = of[...].reshape((S,) + gq.shape[1:]).astype(bf)
    gkv[pl.ds(a * S, S)] = kv[...]
    barrier = pltpu.get_barrier_semaphore()
    for d in range(1, Z):
        pl.semaphore_signal(barrier, 1, device_id={"ffn": (z + d) % Z}, device_id_type=MESH)
    for d in range(1, A):
        pl.semaphore_signal(barrier, 1, device_id={"att": (a + d) % A}, device_id_type=MESH)
    pl.semaphore_wait(barrier, Z - 1 + A - 1)

    def remote(src, dst, ss_, rs_, axis, peer):
        return pltpu.make_async_remote_copy(
            src_ref=src, dst_ref=dst, send_sem=ss_, recv_sem=rs_,
            device_id={axis: peer}, device_id_type=MESH,
        )

    half = z // 2
    inside = z * (Z - 1 - z)
    inner = 1 + half
    outer = 3 * (z - 1)
    other = 3 - z

    def a_copy(j, peer):
        return remote(pa.at[j], ra.at[j], a_ss.at[j], a_rs.at[j], "ffn", peer)

    def m_copy(j):
        return remote(pa.at[j], rm.at[j], m_ss.at[j], m_rs.at[j], "ffn", other)

    def n_copy(j, peer):
        return remote(res.at[j], res.at[j], n_ss.at[j], n_rs.at[j], "ffn", peer)

    def q_copy(hh, d):
        peer = (a + d) % A
        at = hh * (A - 1) + d - 1
        return remote(ss.at[hh, peer], ssr.at[hh, d - 1], q_ss.at[at], q_rs.at[at], "att", peer)

    def c1_copy(hh, k):
        j = hh * NF + k
        return remote(s1.at[j], r1.at[j], c1_ss.at[j], c1_rs.at[j], "att", partner)

    def c2_copy(hh, k):
        j = hh * NF + k
        return remote(s2.at[j], r2.at[j], c2_ss.at[j], c2_rs.at[j], "att", xpeer)

    def h_copy(ss_, rs_, hh, k, block, peer):
        j = hh * NF + k
        return remote(hb.at[j, block], hb.at[j, block], ss_.at[j], rs_.at[j], "att", peer)

    def hp_copy(hh, k, block):
        return h_copy(hp_ss, hp_rs, hh, k, block, partner)

    def hx_copy(hh, k, block):
        return h_copy(hx_ss, hx_rs, hh, k, block, xpeer)

    def hf_copy(hh, k, block):
        return h_copy(hf_ss, hf_rs, hh, k, block, partner)

    def d_copy(hh, n, d):
        peer = (z + d) % Z
        j = hh * NA + n
        return remote(tb.at[hh, peer, n], rd.at[j, d - 1], d_ss.at[j, d - 1], d_rs.at[j, d - 1], "ffn", peer)

    def q_block(i, owner):
        return (gq, gkv)[i].at[pl.ds(owner * S, S)]

    def qx_copy(i, owner):
        return remote(q_block(i, owner), q_block(i, owner), qx_ss.at[i], qx_rs.at[i], "att", xpeer)

    def qp_copy(i, owner):
        return remote(q_block(i, owner), q_block(i, owner), qp_ss.at[i], qp_rs.at[i], "att", partner)

    def qf_copy(i, owner):
        return remote(q_block(i, owner), q_block(i, owner), qf_ss.at[i], qf_rs.at[i], "att", partner)

    for i in range(2):
        qx_copy(i, a).start()
        qp_copy(i, a).start()

    R = slots_row.shape[1]
    shift = S.bit_length() - 1
    cut = HR.bit_length() - 1
    deep = BR.bit_length() - 1
    owned = R // Z

    def request_of(rows):
        piece, owner, own = rows >> cut, (rows >> deep) & (Z - 1), (rows & (BR - 1)) >> 1
        return owner * owned + piece * (BR // STEPS) + own

    spread_row = lax.broadcasted_iota(jnp.int32, (R, R * STEPS), 0)
    spread_col = request_of(lax.broadcasted_iota(jnp.int32, (R, R * STEPS), 1))
    slot_at = jnp.dot(
        jnp.broadcast_to(slots_row[...].astype(f32), (8, R)).astype(bf),
        jnp.where(spread_col == spread_row, 1.0, 0.0).astype(bf),
        preferred_element_type=f32,
    )[:1]
    row = lax.broadcasted_iota(jnp.int32, (R * STEPS, R * STEPS), 0)
    col = lax.broadcasted_iota(jnp.int32, (R * STEPS, R * STEPS), 1)
    low = SG.bit_length() - 1
    side, holder_of = row >> cut, (row >> (low + 1)) & (A - 1)
    row_slot = (holder_of << shift) + (side << low) + (row & (SG - 1))
    row_step = (row >> low) & (STEPS - 1)
    chosen = (row_slot.astype(f32) == slot_at) & (row_step == (col & (STEPS - 1)))
    place[...] = jnp.where(chosen, 1.0, 0.0).astype(bf)

    @pl.loop(0, S)
    def _(i):
        mine = a * S + i
        found = jnp.int32(0)
        for r in range(R):
            found = jnp.where(slots[r] == mine, r, found)
        holders[i] = found

    for i in range(2):
        qx_copy(i, xpeer).wait_recv()
        qf_copy(i, xpeer).start()
    for i in range(2):
        qp_copy(i, partner).wait_recv()
        qf_copy(i, far).wait_recv()

    KB = CAP + 16
    nothing = jnp.zeros((QR, HD), bf)
    scale = HD ** (-0.5)

    def sides(block):
        return (
            jnp.concatenate([block[:, 0:HD], block[:, 2 * HD:3 * HD]], 1),
            jnp.concatenate([block[:, HD:2 * HD], block[:, 3 * HD:4 * HD]], 1),
        )

    def attend(sh):
        everything = []
        for n in range(SG):
            i = sh * SG + n
            rows = gq[holders[i]]
            wide = jnp.concatenate(
                [
                    jnp.concatenate([rows[:QR], nothing], 1),
                    jnp.concatenate([nothing, rows[QR:]], 1),
                ],
                0,
            )
            fresh = gkv[holders[i]].astype(f32)
            fresh = jnp.concatenate(
                [fresh, jnp.zeros((KB - CAP - STEPS, fresh.shape[1]), f32)], 0
            ).astype(bf)
            new_keys, new_values = sides(fresh)
            keys, values = sides(wd_v.at[i // per, kept_rows(i)])
            keys = jnp.concatenate([keys, new_keys], 0)
            scores = lax.dot_general(
                wide, keys, (((1,), (1,)), ((), ())), preferred_element_type=f32
            )
            everything.append((scores, values, new_values))
        weighted = []
        for n in range(SG):
            scores, values, new_values = everything[n]
            length = lengths[sh * SG + n]
            column = lax.broadcasted_iota(jnp.int32, scores.shape, 1)
            step = (lax.broadcasted_iota(jnp.int32, scores.shape, 0) // groups) % STEPS
            seen = (column < length) | ((column >= CAP) & (column <= CAP + step))
            scores = jnp.where(seen, scores * scale, -jnp.inf)
            weights = jnp.exp(scores - jnp.max(scores, -1, keepdims=True))
            total = jnp.sum(weights, -1, keepdims=True)
            weighted.append((weights / total).astype(bf))
        for n in range(SG):
            values = jnp.concatenate(everything[n][1:], 0)
            mixed = jnp.dot(weighted[n], values, preferred_element_type=f32)
            for g in range(kv_local):
                at = (n * kv_local + g) * QR
                of[at:at + QR, :] = mixed[g * QR:(g + 1) * QR, g * HD:(g + 1) * HD]

    def t_copy(sh, ss_, rs_, block, peer):
        return remote(tb.at[sh, block], tb.at[sh, block], ss_.at[sh], rs_.at[sh], "att", peer)

    heads = T // HD
    for i in range(S):
        cache_copy(i).wait()

    for sh in range(2):
        attend(sh)
        for head in range(kv_local * groups):
            g, j = head // groups, head % groups
            both = [
                of[pl.ds(g * QR + t * groups + j, SG, stride=kv_local * QR), :]
                for t in range(STEPS)
            ]
            tb[sh, a, head // heads, :, (head % heads) * HD:(head % heads + 1) * HD] = (
                jnp.concatenate(both, 0).astype(bf)
            )
        t_copy(sh, tx_ss, tx_rs, a, xpeer).start()
        t_copy(sh, tp_ss, tp_rs, a, partner).start()

    for k in range(NA):
        wcopy(wd, wd_v, wd_s, k).start()
    for sh in range(2):
        t_copy(sh, tx_ss, tx_rs, xpeer, xpeer).wait_recv()
        t_copy(sh, tf_ss, tf_rs, xpeer, partner).start()
    sq[...] = jnp.zeros_like(sq)
    in_copy.wait()

    @pl.when(inside > 0)
    def _():
        for owner in range(Z):
            for hh in range(2):
                first_row = hh * HR + owner * BR
                at = owner * owned + hh * (BR // STEPS)
                for j in range(NT):
                    block = kept_in[at:at + BR // STEPS, :, j * TK:(j + 1) * TK]
                    res[j, first_row:first_row + BR, :] = block.reshape(BR, TK)

    for sh in range(2):
        t_copy(sh, tp_ss, tp_rs, partner, partner).wait_recv()
        t_copy(sh, tf_ss, tf_rs, far, partner).wait_recv()
    for k in range(NA):
        attended[:, k * T:(k + 1) * T] = lax.dot_general(
            place[...], tb[:, :, k].reshape(2 * HR, T), (((0,), (0,)), ((), ())),
            preferred_element_type=f32,
        ).astype(bf)

    for i in range(2):
        t_copy(i, tx_ss, tx_rs, a, xpeer).wait_send()
        t_copy(i, tp_ss, tp_rs, a, partner).wait_send()
        t_copy(i, tf_ss, tf_rs, xpeer, partner).wait_send()
    @pl.loop(0, NA)
    def _(k):
        wcopy(wo, wo_v, wo_s, k).wait()
        p = jnp.dot(attended[...], wo_v[k], preferred_element_type=f32).astype(bf)
        for e in range(T // TK):
            j = k * (T // TK) + e
            pa[j] = p[:, e * TK:(e + 1) * TK]

            @pl.when(inside == 0)
            def _():
                a_copy(j, inner).start()

    def add_outer(j):
        a_copy(j, outer).wait_recv()
        pa[j] = (pa[j].astype(f32) + ra[j].astype(f32)).astype(bf)
        m_copy(j).start()

    def add_other(j):
        m_copy(j).wait_recv()
        both = pa[j].astype(f32) + rm[j].astype(f32)
        res[j] = (res[j].astype(f32) + both).astype(bf)
        n_copy(j, outer).start()

    lead = 4

    @pl.when(inside > 0)
    def _():
        @pl.loop(0, lead)
        def _(j):
            add_outer(j)

    def relays(i):
        for e in range(2):
            j = 2 * i + e + lead

            @pl.when((inside > 0) & (j < NT))
            def _():
                add_outer(j)

        for e in range(2):
            @pl.when(inside > 0)
            def _():
                add_other(2 * i + e)

    def normed(i):
        for e in range(2):
            j = 2 * i + e

            @pl.when(inside == 0)
            def _():
                n_copy(j, inner).wait_recv()

            wide = res[j].astype(f32)
            sq[...] += wide * wide
            at = pl.ds(pl.multiple_of(j * TK, TK), TK)
            h[i, :, e * TK:(e + 1) * TK] = (wide * gain[:, at]).astype(bf)

    def send_squares():
        squares = jnp.sum(sq[...], -1, keepdims=True)
        ss[...] = jnp.broadcast_to(squares.reshape(2, A, BR, 1), ss.shape)
        for hh in range(2):
            for d in range(1, A):
                q_copy(hh, d).start()

    def depth(i):
        return pl.ds(pl.multiple_of(i * 2 * TK, 2 * TK), 2 * TK)

    def accumulate(i, fresh=False):
        for n in range(NF):
            for e, w in enumerate((wg_v, wu_v)):
                p = jnp.dot(h[i], w[n, depth(i), :], preferred_element_type=f32)
                p = p.reshape(acc.shape[2:])
                acc[e, n] = p if fresh else acc[e, n] + p

    def first(k):
        i = NK - 1
        for e, w in enumerate((wg_v, wu_v)):
            p = jnp.dot(h[i], w[k, depth(i), :], preferred_element_type=f32)
            acc[e, k] += p.reshape(acc.shape[2:])
            for hh in range(2):
                for xx in range(2):
                    s1[hh * NF + k, e, xx] = acc[e, k, hh, 2 * xx + (1 - c)].astype(bf)
        for hh in range(2):
            c1_copy(hh, k).start()

    def second(hh, k):
        c1_copy(hh, k).wait_recv()
        j = hh * NF + k
        for e in range(2):
            s2[j, e] = (acc[e, k, hh, xpeer] + r1[j, e, 1 - x].astype(f32)).astype(bf)
        c2_copy(hh, k).start()
        for e in range(2):
            acc[e, k, hh, a] += r1[j, e, x].astype(f32)

    def inverse_of(hh):
        total_squares = ss[hh, a]
        for d in range(1, A):
            q_copy(hh, d).wait_recv()
            total_squares = total_squares + ssr[hh, d - 1]
        inv[hh] = lax.rsqrt(total_squares / D + epsilon)

    def third(hh, k):
        c2_copy(hh, k).wait_recv()
        j = hh * NF + k
        inverse = inv[hh, :, :1]
        gate = (acc[0, k, hh, a] + r2[j, 0].astype(f32)) * inverse
        up = (acc[1, k, hh, a] + r2[j, 1].astype(f32)) * inverse
        hb[j, a] = (gate / (1.0 + jnp.exp(-gate)) * up).astype(bf)
        hx_copy(hh, k, a).start()
        hp_copy(hh, k, a).start()

    def fourth(hh, k):
        hx_copy(hh, k, xpeer).wait_recv()
        hf_copy(hh, k, xpeer).start()

    def fifth(hh, k):
        hp_copy(hh, k, partner).wait_recv()
        hf_copy(hh, k, far).wait_recv()

    def down_chunk(hh, n, k):
        at = pl.ds(pl.multiple_of(k * T, T), T)
        return jnp.dot(hb[hh * NF + k].reshape(HR, T), wd_v[n, at, :], preferred_element_type=f32)

    def down_send(hh, n):
        for owner in range(Z):
            tb[hh, owner, n] = acc[0, n, hh, owner].astype(bf)
        for d in range(1, Z):
            d_copy(hh, n, d).start()

    @pl.loop(0, NF)
    def _(k):
        wcopy(wg, wg_v, wg_s, k).wait()
        wcopy(wu, wu_v, wu_s, k).wait()

    relays(0)
    normed(0)
    accumulate(0, True)

    @pl.loop(1, NK - 1)
    def _(i):
        relays(i)
        normed(i)
        accumulate(i)

    relays(NK - 1)
    normed(NK - 1)
    send_squares()
    late = min(2, NF)

    @pl.loop(0, NF)
    def _(k):
        first(k)

        @pl.when(k >= late)
        def _():
            second(0, k - late)

    for k in range(NF - late, NF):
        second(0, k)
    inverse_of(0)

    @pl.loop(0, NF)
    def _(k):
        third(0, k)

    @pl.loop(0, NF)
    def _(k):
        second(1, k)

    @pl.loop(0, NF)
    def _(k):
        fourth(0, k)

    inverse_of(1)

    @pl.loop(0, NF)
    def _(k):
        fifth(0, k)

    for n in range(NA):
        wcopy(wd, wd_v, wd_s, n).wait()
    share = -(-NF // NA)

    @pl.loop(0, NA)
    def _(n):
        p = jnp.zeros((HR, T), f32)
        for k in range(NF):
            p = p + down_chunk(0, n, k)
        acc[0, n, 0] = p.reshape(acc.shape[3:])
        down_send(0, n)

        @pl.loop(n * share, jnp.minimum((n + 1) * share, NF))
        def _(k):
            third(1, k)

    soon = min(2, NF)
    for k in range(soon):
        fourth(1, k)

    def down_step(k, fresh=False):
        fifth(1, k)
        for n in range(NA):
            p = down_chunk(1, n, k).reshape(acc.shape[3:])
            acc[0, n, 1] = p if fresh else acc[0, n, 1] + p

    down_step(0, True)

    @pl.loop(1, NF - 1)
    def _(k):
        @pl.when(k + soon <= NF)
        def _():
            fourth(1, k + soon - 1)

        down_step(k)

    for k in range(max(NF - 2 + soon, 0), NF):
        fourth(1, k)

    fifth(1, NF - 1)

    @pl.loop(0, NA)
    def _(n):
        acc[0, n, 1] += down_chunk(1, n, NF - 1).reshape(acc.shape[3:])
        down_send(1, n)

    for hh in range(2):
        for n in range(NA):
            j = hh * NA + n
            total = acc[0, n, hh, z]
            for d in range(1, Z):
                d_copy(hh, n, d).wait_recv()
                total = total + rd[j, d - 1].astype(f32)
            mine = pl.ds(pl.multiple_of(hh * HR + z * BR, BR), BR)
            parts = T // TK
            kept = [res[n * parts + e, mine, :].astype(f32) for e in range(parts)]
            total = total + jnp.concatenate(kept, -1)
            at = hh * (BR // STEPS)
            out[at:at + BR // STEPS, :, n * T:(n + 1) * T] = total.reshape(
                BR // STEPS, STEPS, T
            ).astype(bf)

    for hh in range(2):
        for n in range(NA):
            for d in range(1, Z):
                d_copy(hh, n, d).wait_send()

    @pl.when(inside == 0)
    def _():
        @pl.loop(0, NT)
        def _(j):
            a_copy(j, inner).wait_send()

    @pl.when(inside > 0)
    def _():
        @pl.loop(0, NT)
        def _(j):
            m_copy(j).wait_send()
            n_copy(j, outer).wait_send()

    for hh in range(2):
        for d in range(1, A):
            q_copy(hh, d).wait_send()
    for i in range(2):
        qx_copy(i, a).wait_send()
        qp_copy(i, a).wait_send()
        qf_copy(i, xpeer).wait_send()
    for hh in range(2):
        @pl.loop(0, NF)
        def _(k):
            c1_copy(hh, k).wait_send()
            c2_copy(hh, k).wait_send()
            hp_copy(hh, k, a).wait_send()
            hx_copy(hh, k, a).wait_send()
            hf_copy(hh, k, xpeer).wait_send()


def fused(slots, lengths, q, kv, incoming, gain, cache, w_out, w_gate, w_up, w_down):
    Z = lax.axis_size("ffn")
    rows, kdim = slots.shape[0] * STEPS, w_out.shape[0]
    width = w_out.shape[1]
    units = w_gate.shape[1]
    T = TILE
    HR = rows // 2
    BR = HR // Z
    TK = 128
    NA, NT, NF = width // T, width // TK, units // T
    AB = rows // 4
    S = cache.shape[0]
    bf, f32 = jnp.bfloat16, jnp.float32
    V = pltpu.VMEM
    dma = pltpu.SemaphoreType.DMA
    vm = pl.BlockSpec(memory_space=pltpu.VMEM)
    sm = pl.BlockSpec(memory_space=pltpu.SMEM)
    hbm = pl.BlockSpec(memory_space=pl.ANY)
    scratch = [
        pltpu.SMEM((S,), jnp.int32), V((rows, rows), bf), V(incoming.shape, bf),
        V((4 * S, STEPS * q.shape[2] // HD, HD), bf), V((4 * S,) + kv.shape[1:], bf),
        V((S * STEPS * q.shape[2] // HD, HD), f32), V((S * STEPS, HD), f32),
        V((2, 4, kdim // T, AB // 2, T), bf), V((rows, kdim), bf),
        V((NA, kdim, T), bf), V((NF, width, T), bf), V((NF, width, T), bf), V((NA, units, T), bf),
        V((NT, rows, TK), bf), V((NT, rows, TK), bf), V((NT, rows, TK), bf), V((NT, rows, TK), bf),
        V((NT // 2, rows, 2 * TK), bf), V((rows, TK), f32), V((2, BR, 128), f32),
        V((2, 4, BR, 128), f32), V((2, 3, BR, 128), f32),
        V((2, NF, 2, 4, BR, T), f32), V((2 * NF, 2, 2, BR, T), bf),
        V((2 * NF, 2, 2, BR, T), bf), V((2 * NF, 2, BR, T), bf),
        V((2 * NF, 2, BR, T), bf), V((2 * NF, 4, BR, T), bf),
        V((2 * NA, Z - 1, BR, T), bf),
        dma((NA,)), dma((NF,)), dma((NF,)), dma((NA,)),
        dma((1,)),
    ] + [dma((NT,)) for _ in range(6)] + [dma((6,)), dma((6,))]
    scratch += [dma((2 * NF,)) for _ in range(10)] + [dma((2 * NA, Z - 1)), dma((2 * NA, Z - 1))]
    scratch += [dma((S,))] + [dma((2,)) for _ in range(6)] + [dma((2,)) for _ in range(6)]
    return pl.pallas_call(
        functools.partial(layer_kernel, (Z, HR, BR, T, TK, NA, NT, NF)),
        out_shape=jax.ShapeDtypeStruct((rows // Z // STEPS, STEPS, width), bf),
        in_specs=[sm, vm, sm, vm, vm, hbm, vm, hbm, hbm, hbm, hbm, hbm],
        out_specs=vm,
        scratch_shapes=scratch,
        compiler_params=pltpu.CompilerParams(
            collective_id=1, has_side_effects=True, vmem_limit_bytes=67043328
        ),
    )(slots, slots[None], lengths, q, kv, incoming, gain, cache, w_out, w_gate, w_up, w_down)


def fits(queries, cache, w_out, w_gate, slot_of):
    slots = cache.shape[0]
    chunks = w_out.shape[1] // TILE
    return (
        lax.axis_size("att") == 4
        and lax.axis_size("ffn") == 4
        and slots % 16 == 0
        and slots & (slots - 1) == 0
        and slot_of.shape[0] == 4 * slots
        and slot_of.shape[0] * STEPS <= 128
        and cache.shape[2] == TILE
        and w_out.shape == (chunks * TILE, chunks * TILE)
        and w_gate.shape[1] % TILE == 0
        and chunks * (w_gate.shape[1] // CAP) >= slots
    )


def local_fused(
    incoming, queries, new_kv, cache, lengths, slot_of, w_out, norm_gain, w_gate, w_up, w_down
):
    return fused(
        slot_of,
        lengths,
        queries,
        new_kv,
        incoming,
        norm_gain[None],
        cache,
        w_out,
        w_gate,
        w_up,
        w_down,
    )


def local(
    incoming, queries, new_kv, cache, lengths, slot_of, w_out, norm_gain, w_gate, w_up, w_down
):
    if fits(queries, cache, w_out, w_gate, slot_of):
        return local_fused(
            incoming, queries, new_kv, cache, lengths, slot_of,
            w_out, norm_gain, w_gate, w_up, w_down,
        )
    ffn_count = lax.axis_size("ffn")
    att_index = lax.axis_index("att")
    ffn_index = lax.axis_index("ffn")
    request_count = slot_of.shape[0]
    slot_count = cache.shape[0]
    kv_local = cache.shape[2] // (2 * HD)
    groups = H // KVH
    score_scale = HD ** (-0.5)
    gathered_q, gathered_kv = (
        lax.all_gather(queries, "att", axis=0, tiled=True),
        lax.all_gather(new_kv, "att", axis=0, tiled=True),
    )
    holders = (
        jnp.zeros((request_count,), jnp.int32)
        .at[slot_of]
        .set(jnp.arange(request_count, dtype=jnp.int32))
    )
    my_requests = lax.dynamic_slice_in_dim(holders, att_index * slot_count, slot_count)
    query_mine = jnp.take(gathered_q, my_requests, axis=0).reshape(
        slot_count, STEPS, kv_local, groups, HD
    )
    fresh_mine = jnp.take(gathered_kv, my_requests, axis=0).reshape(
        slot_count, STEPS, kv_local, 2, HD
    )
    cache_view = cache.reshape(slot_count, CAP, kv_local, 2, HD)
    fresh_scores = (
        jnp.einsum(
            "rskgd,rtkd->rskgt",
            query_mine,
            fresh_mine[:, :, :, 0],
            preferred_element_type=jnp.float32,
        )
        * score_scale
    )
    causal = jnp.arange(STEPS)[None, :] <= jnp.arange(STEPS)[:, None]
    fresh_scores = jnp.where(causal[None, :, None, None, :], fresh_scores, -jnp.inf)
    kept_scores = (
        jnp.einsum(
            "rskgd,rckd->rskgc",
            query_mine,
            cache_view[:, :, :, 0],
            preferred_element_type=jnp.float32,
        )
        * score_scale
    )
    in_range = jnp.arange(CAP)[None, :] < lengths[:, None]
    kept_scores = jnp.where(in_range[:, None, None, None, :], kept_scores, -jnp.inf)
    top_score = jnp.maximum(jnp.max(kept_scores, -1), jnp.max(fresh_scores, -1))
    kept_exp = jnp.exp(kept_scores - top_score[..., None])
    fresh_exp = jnp.exp(fresh_scores - top_score[..., None])
    denominator = jnp.sum(kept_exp, -1) + jnp.sum(fresh_exp, -1)
    kept_prob = (kept_exp / denominator[..., None]).astype(jnp.bfloat16)
    fresh_prob = (fresh_exp / denominator[..., None]).astype(jnp.bfloat16)
    mixture = jnp.einsum(
        "rskgc,rckd->rskgd", kept_prob, cache_view[:, :, :, 1], preferred_element_type=jnp.float32
    )
    mixture = mixture + jnp.einsum(
        "rskgt,rtkd->rskgd", fresh_prob, fresh_mine[:, :, :, 1], preferred_element_type=jnp.float32
    )
    attended = mixture.astype(jnp.bfloat16).reshape(slot_count, STEPS, kv_local * groups * HD)
    shard_rows = lax.all_gather(attended, "att", axis=0, tiled=True)
    row_count = shard_rows.shape[0]
    flattened = shard_rows.reshape(row_count * STEPS, shard_rows.shape[2])
    heads_slots = jnp.dot(flattened, w_out, preferred_element_type=jnp.float32).reshape(
        row_count, STEPS, w_out.shape[1]
    )
    heads_requests = jnp.take(heads_slots, slot_of, axis=0)
    heads_total = lax.psum(heads_requests, "ffn")
    residual = (incoming.astype(jnp.float32) + heads_total).astype(jnp.bfloat16)
    residual_wide = residual.astype(jnp.float32)
    squares = lax.psum(jnp.sum(residual_wide * residual_wide, -1), "att")
    normed = (residual_wide * lax.rsqrt(squares / D + epsilon)[..., None] * norm_gain).astype(
        jnp.bfloat16
    )
    normed = normed.reshape(request_count * STEPS, normed.shape[2])
    gate_term = jnp.dot(normed, w_gate, preferred_element_type=jnp.float32)
    upward_term = jnp.dot(normed, w_up, preferred_element_type=jnp.float32)
    unit_share = lax.psum_scatter(
        jnp.concatenate([gate_term, upward_term], 1), "att", scatter_dimension=0, tiled=True
    )
    unit_width = w_gate.shape[1]
    hidden_share = (jax.nn.silu(unit_share[:, :unit_width]) * unit_share[:, unit_width:]).astype(
        jnp.bfloat16
    )
    down_part = jnp.dot(
        lax.all_gather(hidden_share, "att", axis=0, tiled=True),
        w_down,
        preferred_element_type=jnp.float32,
    )
    out_share = lax.psum_scatter(down_part, "ffn", scatter_dimension=0, tiled=True)
    row_share = request_count // ffn_count
    own_state = lax.dynamic_slice_in_dim(residual_wide, ffn_index * row_share, row_share, 0)
    return (own_state + out_share.reshape(row_share, STEPS, out_share.shape[1])).astype(
        jnp.bfloat16
    )


def solution(mesh):
    return jax.shard_map(
        local,
        mesh=mesh,
        in_specs=(
            P("parts", None, "att"),
            P(("parts", "att"), None, "ffn"),
            P(("parts", "att"), None, "ffn"),
            P(("parts", "att"), None, "ffn"),
            P(("parts", "att")),
            P("parts"),
            P("ffn", "att"),
            P("att"),
            P("att", "ffn"),
            P("att", "ffn"),
            P("ffn", "att"),
        ),
        out_specs=P(("parts", "ffn"), None, "att"),
        check_vma=False,
    )
```

time: 86.7 us -> 74.3 us (0.86)
  Pallas kernels: 81.9 us -> 72.5 us
  local copies, waits for them, and re-layouts: 3.32 us -> 1.65 us
  other arithmetic: 1.34 us -> 0 us
    pallas_call x1, Pallas kernels: 81.9 us -> 72.5 us  [fused(): pl.pallas_call(functools.partial(layer_kernel, (Z, HR, BR, T, TK, NA, NT,...]
    reshape x2 -> x0, local copies, waits for them, and re-layouts: 1.66 us -> none  [local_fused(): queries.reshape(slots, STEPS, kv_local, groups, HD).transpose(0, 2, 1, 3, 4)]
    reduce_sum x1 -> x0, other arithmetic: 1.34 us -> none  [local_fused(): jnp.sum(jnp.where(held, requests[None, :], 0), 1)]
where the time goes in v2:
time: 74.3 us; the launch traced here: 74.1 us
  Pallas kernels  72.5 us (98%)
  local copies, waits for them, and re-layouts  1.65 us (2%)
    pallas_call x1, Pallas kernels, fused(): pl.pallas_call(functools.partial(layer_kernel, (Z, HR, BR, T, TK, NA, NT,...  72.5 us
    unnamed x1, local copies, waits for them, and re-layouts  1.65 us

profile of v2, /device:TPU:0, one launch (start us, length us, event | category | flops | bytes accessed | tf_op | source)
XLA Modules:
  0.0 74.1 jit_solution(15220077400600727267)
XLA Ops:
  0.0 72.5 %shard_map.109 = bf16[16,2,2048]{2,1,0:T(2,128)(2,1)} custom-call(s32[64]{0:T(128)} %slots.1, s32[1,64]{1,0:T(1,128)} %bitcast.3, s32[16]{0:T(128)} %lengths.1, bf16[16,2,2048]{2,1,0:T(2,128)(2,1)} %q.1, bf16[16,2,512]{2,1,0:T(2,128)(2,1)} %kv.1, bf16[64,2,2048]{2,1,0:T(2,128)(2,1)} %incoming.1, f32[1,2048]{1,0:T(1,128)} %bitcast.2, ...), custom_call_target="tpu_custom_call" | custom-call | tf_op jit(solution)/shard_map/pallas_call | solution.py:619
  72.5 1.7 %copy.13 = bf16[16,2,2048]{2,1,0:T(2,128)(2,1)} copy(bf16[16,2,2048]{2,1,0:T(2,128)(2,1)} %shard_map.109) | data formatting | bytes 262144

commit v3 on v2

--- a/solution.py
+++ b/solution.py
@@ -25,7 +25,7 @@
     holders, place, kept_in, gq, gkv, of, pair, tb, attended,
     wo_v, wg_v, wu_v, wd_v,
     pa, ra, rm, res, h, sq, inv, ss, ssr,
-    acc, s1, r1, s2, r2, hb,
+    acc, s1, r1, s2, o2, r2, hb,
     rd,
     wo_s, wg_s, wu_s, wd_s,
     in_s, a_ss, a_rs, m_ss, m_rs, n_ss, n_rs, q_ss, q_rs,
@@ -35,8 +35,8 @@
     cache_s, qp_ss, qp_rs, qx_ss, qx_rs, qf_ss, qf_rs,
     tp_ss, tp_rs, tx_ss, tx_rs, tf_ss, tf_rs,
 ):
-    Z, HR, BR, T, TK, NA, NT, NF = cfg
-    NK = NT // 2
+    Z, HR, BR, T, TK, NA, NK, NF = cfg
+    NT = 2 * NK
     S = cache.shape[0]
     kv_local = cache.shape[2] // (2 * HD)
     groups = H // KVH
@@ -283,13 +283,12 @@
 
     @pl.when(inside > 0)
     def _():
-        for owner in range(Z):
-            for hh in range(2):
-                first_row = hh * HR + owner * BR
+        for j in range(NT):
+            hh, k = j // NK, j % NK
+            for owner in range(Z):
                 at = owner * owned + hh * (BR // STEPS)
-                for j in range(NT):
-                    block = kept_in[at:at + BR // STEPS, :, j * TK:(j + 1) * TK]
-                    res[j, first_row:first_row + BR, :] = block.reshape(BR, TK)
+                block = kept_in[at:at + BR // STEPS, :, k * TK:(k + 1) * TK]
+                res[j, owner * BR:(owner + 1) * BR, :] = block.reshape(BR, TK)
 
     for sh in range(2):
         t_copy(sh, tp_ss, tp_rs, partner, partner).wait_recv()
@@ -304,17 +303,28 @@
         t_copy(i, tx_ss, tx_rs, a, xpeer).wait_send()
         t_copy(i, tp_ss, tp_rs, a, partner).wait_send()
         t_copy(i, tf_ss, tf_rs, xpeer, partner).wait_send()
-    @pl.loop(0, NA)
+    @pl.loop(0, NK)
     def _(k):
-        wcopy(wo, wo_v, wo_s, k).wait()
-        p = jnp.dot(attended[...], wo_v[k], preferred_element_type=f32).astype(bf)
-        for e in range(T // TK):
-            j = k * (T // TK) + e
-            pa[j] = p[:, e * TK:(e + 1) * TK]
-
-            @pl.when(inside == 0)
-            def _():
-                a_copy(j, inner).start()
+        parts = T // TK
+
+        @pl.when(k % parts == 0)
+        def _():
+            wcopy(wo, wo_v, wo_s, k // parts).wait()
+
+        at = pl.ds(pl.multiple_of((k % parts) * TK, TK), TK)
+        p = jnp.dot(attended[...], wo_v[k // parts, :, at], preferred_element_type=f32).astype(bf)
+        for hh in range(2):
+            pa[hh * NK + k] = p[hh * HR:(hh + 1) * HR]
+
+        @pl.when(inside == 0)
+        def _():
+            a_copy(k, inner).start()
+
+    @pl.when(inside == 0)
+    def _():
+        @pl.loop(NK, NT)
+        def _(j):
+            a_copy(j, inner).start()
 
     def add_outer(j):
         a_copy(j, outer).wait_recv()
@@ -327,76 +337,55 @@
         res[j] = (res[j].astype(f32) + both).astype(bf)
         n_copy(j, outer).start()
 
-    lead = 4
-
-    @pl.when(inside > 0)
-    def _():
-        @pl.loop(0, lead)
-        def _(j):
-            add_outer(j)
-
-    def relays(i):
-        for e in range(2):
-            j = 2 * i + e + lead
-
-            @pl.when((inside > 0) & (j < NT))
-            def _():
-                add_outer(j)
-
-        for e in range(2):
-            @pl.when(inside > 0)
-            def _():
-                add_other(2 * i + e)
-
-    def normed(i):
-        for e in range(2):
-            j = 2 * i + e
-
-            @pl.when(inside == 0)
-            def _():
-                n_copy(j, inner).wait_recv()
-
-            wide = res[j].astype(f32)
-            sq[...] += wide * wide
-            at = pl.ds(pl.multiple_of(j * TK, TK), TK)
-            h[i, :, e * TK:(e + 1) * TK] = (wide * gain[:, at]).astype(bf)
-
-    def send_squares():
-        squares = jnp.sum(sq[...], -1, keepdims=True)
-        ss[...] = jnp.broadcast_to(squares.reshape(2, A, BR, 1), ss.shape)
-        for hh in range(2):
-            for d in range(1, A):
-                q_copy(hh, d).start()
+    def normed(hh, i):
+        j = hh * NK + i
+
+        @pl.when(inside == 0)
+        def _():
+            n_copy(j, inner).wait_recv()
+
+        wide = res[j].astype(f32)
+        square = wide * wide
+        for e in range(TK // 128):
+            sq[hh] += square[:, e * 128:(e + 1) * 128]
+        at = pl.ds(pl.multiple_of(i * TK, TK), TK)
+        h[j] = (wide * gain[:, at]).astype(bf)
+
+    def send_squares(hh):
+        squares = jnp.sum(sq[hh], -1, keepdims=True)
+        ss[hh] = jnp.broadcast_to(squares.reshape(A, BR, 1), ss.shape[1:])
+        for d in range(1, A):
+            q_copy(hh, d).start()
 
     def depth(i):
-        return pl.ds(pl.multiple_of(i * 2 * TK, 2 * TK), 2 * TK)
-
-    def accumulate(i, fresh=False):
-        for n in range(NF):
+        return pl.ds(pl.multiple_of(i * TK, TK), TK)
+
+    def accumulate(hh, i, fresh=False, units=range(NF)):
+        for n in units:
             for e, w in enumerate((wg_v, wu_v)):
-                p = jnp.dot(h[i], w[n, depth(i), :], preferred_element_type=f32)
+                p = jnp.dot(h[hh * NK + i], w[n, depth(i), :], preferred_element_type=f32)
                 p = p.reshape(acc.shape[2:])
                 acc[e, n] = p if fresh else acc[e, n] + p
 
-    def first(k):
+    def first(hh, ks):
         i = NK - 1
-        for e, w in enumerate((wg_v, wu_v)):
-            p = jnp.dot(h[i], w[k, depth(i), :], preferred_element_type=f32)
-            acc[e, k] += p.reshape(acc.shape[2:])
-            for hh in range(2):
+        for k in ks:
+            for e, w in enumerate((wg_v, wu_v)):
+                p = jnp.dot(h[hh * NK + i], w[k, depth(i), :], preferred_element_type=f32)
+                acc[e, k] += p.reshape(acc.shape[2:])
+        for k in ks:
+            for e in range(2):
                 for xx in range(2):
-                    s1[hh * NF + k, e, xx] = acc[e, k, hh, 2 * xx + (1 - c)].astype(bf)
-        for hh in range(2):
+                    s1[hh * NF + k, e, xx] = acc[e, k, 2 * xx + (1 - c)].astype(bf)
             c1_copy(hh, k).start()
 
     def second(hh, k):
         c1_copy(hh, k).wait_recv()
         j = hh * NF + k
         for e in range(2):
-            s2[j, e] = (acc[e, k, hh, xpeer] + r1[j, e, 1 - x].astype(f32)).astype(bf)
+            s2[j, e] = (acc[e, k, xpeer] + r1[j, e, 1 - x].astype(f32)).astype(bf)
+            o2[j, e] = acc[e, k, a] + r1[j, e, x].astype(f32)
         c2_copy(hh, k).start()
-        for e in range(2):
-            acc[e, k, hh, a] += r1[j, e, x].astype(f32)
 
     def inverse_of(hh):
         total_squares = ss[hh, a]
@@ -409,8 +398,8 @@
         c2_copy(hh, k).wait_recv()
         j = hh * NF + k
         inverse = inv[hh, :, :1]
-        gate = (acc[0, k, hh, a] + r2[j, 0].astype(f32)) * inverse
-        up = (acc[1, k, hh, a] + r2[j, 1].astype(f32)) * inverse
+        gate = (o2[j, 0] + r2[j, 0].astype(f32)) * inverse
+        up = (o2[j, 1] + r2[j, 1].astype(f32)) * inverse
         hb[j, a] = (gate / (1.0 + jnp.exp(-gate)) * up).astype(bf)
         hx_copy(hh, k, a).start()
         hp_copy(hh, k, a).start()
@@ -429,85 +418,151 @@
 
     def down_send(hh, n):
         for owner in range(Z):
-            tb[hh, owner, n] = acc[0, n, hh, owner].astype(bf)
+            tb[hh, owner, n] = acc[1 - hh, n, owner].astype(bf)
         for d in range(1, Z):
             d_copy(hh, n, d).start()
+
+    late = min(2, NF)
 
     @pl.loop(0, NF)
     def _(k):
         wcopy(wg, wg_v, wg_s, k).wait()
         wcopy(wu, wu_v, wu_s, k).wait()
 
-    relays(0)
-    normed(0)
-    accumulate(0, True)
+    def advance(hh, i, fresh=False):
+        normed(hh, i)
+        accumulate(hh, i, fresh)
+
+    @pl.when(inside == 0)
+    def _():
+        advance(0, 0, True)
+
+        @pl.loop(1, NK - 1)
+        def _(i):
+            advance(0, i)
+
+    @pl.when(inside > 0)
+    def _():
+        @pl.loop(0, 6)
+        def _(j):
+            add_outer(j)
+
+        for j in range(2):
+            add_other(j)
+        advance(0, 0, True)
+
+        @pl.loop(1, NK // 2)
+        def _(i):
+            @pl.when(i < 3)
+            def _():
+                for e in range(2):
+                    add_outer(2 * i + 4 + e)
+
+            @pl.when(i == 2)
+            def _():
+                add_outer(10)
+
+            @pl.when(i == 3)
+            def _():
+                for j in range(11, 14):
+                    add_outer(j)
+
+            for e in range(2):
+                add_other(2 * i + e)
+            for e in range(2):
+                advance(0, 2 * i - 1 + e)
+
+        for j in range(14, NT):
+            add_outer(j)
+
+    normed(0, NK - 1)
+    send_squares(0)
+    bundles = ((0,), (1, 2), (3, 4), (5, 6))
+    for at, ks in enumerate(bundles):
+        first(0, ks)
+        if at > 1:
+            for k in bundles[at - 2]:
+                second(0, k)
+
+        @pl.when(inside > 0)
+        def _():
+            for k in ks:
+                add_other(NK + k)
+
+    for k in bundles[2]:
+        second(0, k)
+
+    @pl.when(inside > 0)
+    def _():
+        for j in range(NK + NF, NT):
+            add_other(j)
+
+    normed(1, 0)
+    accumulate(1, 0, True, range(bundles[3][0]))
+    for k in bundles[3]:
+        second(0, k)
+    accumulate(1, 0, True, bundles[3])
+    inverse_of(0)
 
     @pl.loop(1, NK - 1)
     def _(i):
-        relays(i)
-        normed(i)
-        accumulate(i)
-
-    relays(NK - 1)
-    normed(NK - 1)
-    send_squares()
-    late = min(2, NF)
-
-    @pl.loop(0, NF)
-    def _(k):
-        first(k)
-
-        @pl.when(k >= late)
+        advance(1, i)
+
+        @pl.when(i == 3)
         def _():
-            second(0, k - late)
-
-    for k in range(NF - late, NF):
-        second(0, k)
-    inverse_of(0)
-
-    @pl.loop(0, NF)
-    def _(k):
+            third(0, 0)
+
+        @pl.when(i >= 3)
+        def _():
+            third(0, i - 2)
+
+    for k in range(NK - 3, NF):
         third(0, k)
-
-    @pl.loop(0, NF)
-    def _(k):
+    normed(1, NK - 1)
+    send_squares(1)
+    for at, ks in enumerate(bundles):
+        first(1, ks)
+        if at > 0:
+            for k in bundles[at - 1]:
+                second(1, k)
+        for k in bundles[at]:
+            if k < 4:
+                fourth(0, k)
+    for k in bundles[-1]:
         second(1, k)
-
-    @pl.loop(0, NF)
-    def _(k):
+    for k in range(4, NF):
         fourth(0, k)
-
     inverse_of(1)
 
     @pl.loop(0, NF)
     def _(k):
         fifth(0, k)
 
+    share = -(-NF // NA)
     for n in range(NA):
         wcopy(wd, wd_v, wd_s, n).wait()
-    share = -(-NF // NA)
 
     @pl.loop(0, NA)
     def _(n):
         p = jnp.zeros((HR, T), f32)
         for k in range(NF):
             p = p + down_chunk(0, n, k)
-        acc[0, n, 0] = p.reshape(acc.shape[3:])
+        acc[1, n] = p.reshape(acc.shape[2:])
         down_send(0, n)
 
         @pl.loop(n * share, jnp.minimum((n + 1) * share, NF))
         def _(k):
             third(1, k)
 
-    soon = min(2, NF)
+    soon = min(3, NF)
     for k in range(soon):
         fourth(1, k)
 
     def down_step(k, fresh=False):
         fifth(1, k)
         for n in range(NA):
-            p = down_chunk(1, n, k).reshape(acc.shape[3:])
-            acc[0, n, 1] = p if fresh else acc[0, n, 1] + p
+            p = down_chunk(1, n, k).reshape(acc.shape[2:])
+            acc[0, n] = p if fresh else acc[0, n] + p
 
     down_step(0, True)
 
@@ -526,19 +581,19 @@
 
     @pl.loop(0, NA)
     def _(n):
-        acc[0, n, 1] += down_chunk(1, n, NF - 1).reshape(acc.shape[3:])
+        acc[0, n] += down_chunk(1, n, NF - 1).reshape(acc.shape[2:])
         down_send(1, n)
 
     for hh in range(2):
         for n in range(NA):
             j = hh * NA + n
-            total = acc[0, n, hh, z]
+            total = acc[1 - hh, n, z]
             for d in range(1, Z):
                 d_copy(hh, n, d).wait_recv()
                 total = total + rd[j, d - 1].astype(f32)
-            mine = pl.ds(pl.multiple_of(hh * HR + z * BR, BR), BR)
+            mine = pl.ds(pl.multiple_of(z * BR, BR), BR)
             parts = T // TK
-            kept = [res[n * parts + e, mine, :].astype(f32) for e in range(parts)]
+            kept = [res[hh * NK + n * parts + e, mine, :].astype(f32) for e in range(parts)]
             total = total + jnp.concatenate(kept, -1)
             at = hh * (BR // STEPS)
             out[at:at + BR // STEPS, :, n * T:(n + 1) * T] = total.reshape(
@@ -588,8 +643,8 @@
     T = TILE
     HR = rows // 2
     BR = HR // Z
-    TK = 128
-    NA, NT, NF = width // T, width // TK, units // T
+    TK = T // 2
+    NA, NK, NF = width // T, width // TK, units // T
     AB = rows // 4
     S = cache.shape[0]
     bf, f32 = jnp.bfloat16, jnp.float32
@@ -604,20 +659,20 @@
         V((S * STEPS * q.shape[2] // HD, HD), f32), V((S * STEPS, HD), f32),
         V((2, 4, kdim // T, AB // 2, T), bf), V((rows, kdim), bf),
         V((NA, kdim, T), bf), V((NF, width, T), bf), V((NF, width, T), bf), V((NA, units, T), bf),
-        V((NT, rows, TK), bf), V((NT, rows, TK), bf), V((NT, rows, TK), bf), V((NT, rows, TK), bf),
-        V((NT // 2, rows, 2 * TK), bf), V((rows, TK), f32), V((2, BR, 128), f32),
+        V((2 * NK, HR, TK), bf), V((2 * NK, HR, TK), bf), V((2 * NK, HR, TK), bf), V((2 * NK, HR, TK), bf),
+        V((2 * NK, HR, TK), bf), V((2, HR, 128), f32), V((2, BR, 128), f32),
         V((2, 4, BR, 128), f32), V((2, 3, BR, 128), f32),
-        V((2, NF, 2, 4, BR, T), f32), V((2 * NF, 2, 2, BR, T), bf),
-        V((2 * NF, 2, 2, BR, T), bf), V((2 * NF, 2, BR, T), bf),
+        V((2, NF, 4, BR, T), f32), V((2 * NF, 2, 2, BR, T), bf),
+        V((2 * NF, 2, 2, BR, T), bf), V((2 * NF, 2, BR, T), bf), V((2 * NF, 2, BR, T), f32),
         V((2 * NF, 2, BR, T), bf), V((2 * NF, 4, BR, T), bf),
         V((2 * NA, Z - 1, BR, T), bf),
         dma((NA,)), dma((NF,)), dma((NF,)), dma((NA,)),
         dma((1,)),
-    ] + [dma((NT,)) for _ in range(6)] + [dma((6,)), dma((6,))]
+    ] + [dma((2 * NK,)) for _ in range(6)] + [dma((6,)), dma((6,))]
     scratch += [dma((2 * NF,)) for _ in range(10)] + [dma((2 * NA, Z - 1)), dma((2 * NA, Z - 1))]
     scratch += [dma((S,))] + [dma((2,)) for _ in range(6)] + [dma((2,)) for _ in range(6)]
     return pl.pallas_call(
-        functools.partial(layer_kernel, (Z, HR, BR, T, TK, NA, NT, NF)),
+        functools.partial(layer_kernel, (Z, HR, BR, T, TK, NA, NK, NF)),
         out_shape=jax.ShapeDtypeStruct((rows // Z // STEPS, STEPS, width), bf),
         in_specs=[sm, vm, sm, vm, vm, hbm, vm, hbm, hbm, hbm, hbm, hbm],
         out_specs=vm,
@@ -639,8 +694,9 @@
         and slot_of.shape[0] == 4 * slots
         and slot_of.shape[0] * STEPS <= 128
         and cache.shape[2] == TILE
+        and chunks == 4
         and w_out.shape == (chunks * TILE, chunks * TILE)
-        and w_gate.shape[1] % TILE == 0
+        and w_gate.shape[1] == 7 * TILE
         and chunks * (w_gate.shape[1] // CAP) >= slots
     )
 

time: 74.3 us -> 70.3 us (0.946)
  Pallas kernels: 72.5 us -> 68.5 us
    pallas_call x1, Pallas kernels: 72.5 us -> 68.5 us  [fused(): pl.pallas_call(functools.partial(layer_kernel, (Z, HR, BR, T, TK, NA, NK,...]
where the time goes in v3:
time: 70.3 us; the launch traced here: 70.2 us
  Pallas kernels  68.5 us (97%)
  local copies, waits for them, and re-layouts  1.65 us (2%)
    pallas_call x1, Pallas kernels, fused(): pl.pallas_call(functools.partial(layer_kernel, (Z, HR, BR, T, TK, NA, NK,...  68.5 us
    unnamed x1, local copies, waits for them, and re-layouts  1.65 us

profile of v3, /device:TPU:0, one launch (start us, length us, event | category | flops | bytes accessed | tf_op | source)
XLA Modules:
  0.0 70.2 jit_solution(1430856150728086497)
XLA Ops:
  0.0 68.5 %shard_map.109 = bf16[16,2,2048]{2,1,0:T(2,128)(2,1)} custom-call(s32[64]{0:T(128)} %slots.1, s32[1,64]{1,0:T(1,128)} %bitcast.3, s32[16]{0:T(128)} %lengths.1, bf16[16,2,2048]{2,1,0:T(2,128)(2,1)} %q.1, bf16[16,2,512]{2,1,0:T(2,128)(2,1)} %kv.1, bf16[64,2,2048]{2,1,0:T(2,128)(2,1)} %incoming.1, f32[1,2048]{1,0:T(1,128)} %bitcast.2, ...), custom_call_target="tpu_custom_call" | custom-call | tf_op jit(solution)/shard_map/pallas_call | solution.py:674
  68.5 1.7 %copy.13 = bf16[16,2,2048]{2,1,0:T(2,128)(2,1)} copy(bf16[16,2,2048]{2,1,0:T(2,128)(2,1)} %shard_map.109) | data formatting | bytes 262144

commit v4 on v3

--- a/solution.py
+++ b/solution.py
@@ -22,11 +22,11 @@
 
 def layer_kernel(
     cfg, slots, slots_row, lengths, q, kv, incoming, gain, cache, wo, wg, wu, wd, out,
-    holders, place, kept_in, gq, gkv, of, pair, tb, attended,
+    holders, place, kept_in, gq_a, gkv_a, gq_b, gkv_b, of, pair, tb, attended,
     wo_v, wg_v, wu_v, wd_v,
     pa, ra, rm, res, h, sq, inv, ss, ssr,
     acc, s1, r1, s2, o2, r2, hb,
-    rd,
+    rd, result, out_s,
     wo_s, wg_s, wu_s, wd_s,
     in_s, a_ss, a_rs, m_ss, m_rs, n_ss, n_rs, q_ss, q_rs,
     c1_ss, c1_rs, c2_ss, c2_rs,
@@ -51,10 +51,13 @@
     far = 2 * (1 - x) + (1 - c)
     bf, f32 = jnp.bfloat16, jnp.float32
 
-    def wcopy(src, dst, sem, k):
+    def wcopy(src, dst, sem, k, at=0):
         return pltpu.make_async_copy(
-            src.at[:, pl.ds(pl.multiple_of(k * T, T), T)], dst.at[k], sem.at[k]
+            src.at[:, pl.ds(pl.multiple_of(k * T, T), T)], dst.at[k], sem.at[at]
         )
+
+    def wait_bytes(ref, sem):
+        pltpu.make_async_copy(ref, ref, sem).wait()
 
     def kept_rows(i):
         return pl.ds(pl.multiple_of((i % per) * CAP, CAP), CAP)
@@ -69,7 +72,7 @@
     in_copy = pltpu.make_async_copy(incoming, kept_in, in_s.at[0])
     in_copy.start()
     for k in range(NA):
-        wcopy(wo, wo_v, wo_s, k).start()
+        wcopy(wo, wo_v, wo_s, k, k).start()
     for k in range(NF):
         wcopy(wg, wg_v, wg_s, k).start()
         wcopy(wu, wu_v, wu_s, k).start()
@@ -80,11 +83,14 @@
         block = q[:, :, head * HD:(head + 1) * HD].astype(f32)
         pair[...] = block.reshape(pair.shape)
         for t in range(STEPS):
-            of[pl.ds(g * QR + t * groups + j, S, stride=kv_local * QR), :] = pair[
+            of[pl.ds(g * S * QR + t * groups + j, S, stride=QR), :] = pair[
                 pl.ds(t, S, stride=STEPS), :
             ]
-    gq[pl.ds(a * S, S)] = of[...].reshape((S,) + gq.shape[1:]).astype(bf)
-    gkv[pl.ds(a * S, S)] = kv[...]
+    gq, gkv = (gq_a, gq_b), (gkv_a, gkv_b)
+    for g in range(kv_local):
+        rows = of[g * S * QR:(g + 1) * S * QR, :]
+        gq[g][pl.ds(a * S, S)] = rows.reshape((S,) + gq[g].shape[1:]).astype(bf)
+        gkv[g][pl.ds(a * S, S)] = kv[:, :, g * 2 * HD:(g + 1) * 2 * HD]
     barrier = pltpu.get_barrier_semaphore()
     for d in range(1, Z):
         pl.semaphore_signal(barrier, 1, device_id={"ffn": (z + d) % Z}, device_id_type=MESH)
@@ -105,58 +111,64 @@
     other = 3 - z
 
     def a_copy(j, peer):
-        return remote(pa.at[j], ra.at[j], a_ss.at[j], a_rs.at[j], "ffn", peer)
+        return remote(pa.at[j], ra.at[j], a_ss.at[0], a_rs.at[j], "ffn", peer)
 
     def m_copy(j):
-        return remote(pa.at[j], rm.at[j], m_ss.at[j], m_rs.at[j], "ffn", other)
+        return remote(pa.at[j], rm.at[j], m_ss.at[0], m_rs.at[j], "ffn", other)
 
     def n_copy(j, peer):
-        return remote(res.at[j], res.at[j], n_ss.at[j], n_rs.at[j], "ffn", peer)
+        return remote(res.at[j], res.at[j], n_ss.at[0], n_rs.at[j], "ffn", peer)
 
     def q_copy(hh, d):
         peer = (a + d) % A
-        at = hh * (A - 1) + d - 1
-        return remote(ss.at[hh, peer], ssr.at[hh, d - 1], q_ss.at[at], q_rs.at[at], "att", peer)
+        return remote(ss.at[hh, peer], ssr.at[hh, d - 1], q_ss.at[d - 1], q_rs.at[hh], "att", peer)
 
     def c1_copy(hh, k):
         j = hh * NF + k
-        return remote(s1.at[j], r1.at[j], c1_ss.at[j], c1_rs.at[j], "att", partner)
+        return remote(s1.at[j], r1.at[j], c1_ss.at[0], c1_rs.at[j], "att", partner)
 
     def c2_copy(hh, k):
         j = hh * NF + k
-        return remote(s2.at[j], r2.at[j], c2_ss.at[j], c2_rs.at[j], "att", xpeer)
-
-    def h_copy(ss_, rs_, hh, k, block, peer):
+        return remote(s2.at[j], r2.at[j], c2_ss.at[0], c2_rs.at[j], "att", far)
+
+    def h_copy(ss_, rs_, at, hh, k, block, peer):
         j = hh * NF + k
-        return remote(hb.at[j, block], hb.at[j, block], ss_.at[j], rs_.at[j], "att", peer)
+        return remote(hb.at[j, block], hb.at[j, block], ss_.at[0], rs_.at[at], "att", peer)
+
+    def late_at(hh, k):
+        return 0 if hh == 0 else 1 + k
 
     def hp_copy(hh, k, block):
-        return h_copy(hp_ss, hp_rs, hh, k, block, partner)
+        return h_copy(hp_ss, hp_rs, late_at(hh, k), hh, k, block, partner)
 
     def hx_copy(hh, k, block):
-        return h_copy(hx_ss, hx_rs, hh, k, block, xpeer)
+        return h_copy(hx_ss, hx_rs, hh * NF + k, hh, k, block, far)
 
     def hf_copy(hh, k, block):
-        return h_copy(hf_ss, hf_rs, hh, k, block, partner)
+        return h_copy(hf_ss, hf_rs, late_at(hh, k), hh, k, block, partner)
 
     def d_copy(hh, n, d):
         peer = (z + d) % Z
         j = hh * NA + n
-        return remote(tb.at[hh, peer, n], rd.at[j, d - 1], d_ss.at[j, d - 1], d_rs.at[j, d - 1], "ffn", peer)
+        return remote(tb.at[hh, peer, n], rd.at[j, d - 1], d_ss.at[d - 1], d_rs.at[late_at(hh, n)], "ffn", peer)
 
     def q_block(i, owner):
-        return (gq, gkv)[i].at[pl.ds(owner * S, S)]
+        return (gq, gkv)[i % 2][i // 2].at[pl.ds(owner * S, S)]
+
+    def q_copy_of(ss_, rs_, i, owner, peer):
+        block = q_block(i, owner)
+        return remote(block, block, ss_.at[i], rs_.at[i], "att", peer)
 
     def qx_copy(i, owner):
-        return remote(q_block(i, owner), q_block(i, owner), qx_ss.at[i], qx_rs.at[i], "att", xpeer)
+        return q_copy_of(qx_ss, qx_rs, i, owner, far)
 
     def qp_copy(i, owner):
-        return remote(q_block(i, owner), q_block(i, owner), qp_ss.at[i], qp_rs.at[i], "att", partner)
+        return q_copy_of(qp_ss, qp_rs, i, owner, partner)
 
     def qf_copy(i, owner):
-        return remote(q_block(i, owner), q_block(i, owner), qf_ss.at[i], qf_rs.at[i], "att", partner)
-
-    for i in range(2):
+        return q_copy_of(qf_ss, qf_rs, i, owner, partner)
+
+    for i in range(2 * kv_local):
         qx_copy(i, a).start()
         qp_copy(i, a).start()
 
@@ -194,90 +206,95 @@
             found = jnp.where(slots[r] == mine, r, found)
         holders[i] = found
 
-    for i in range(2):
-        qx_copy(i, xpeer).wait_recv()
-        qf_copy(i, xpeer).start()
-    for i in range(2):
-        qp_copy(i, partner).wait_recv()
-        qf_copy(i, far).wait_recv()
-
+    def pass_queries(g):
+        for i in (2 * g, 2 * g + 1):
+            qx_copy(i, far).wait_recv()
+            qf_copy(i, far).start()
+
+    def have_queries(g):
+        for i in (2 * g, 2 * g + 1):
+            qp_copy(i, partner).wait_recv()
+            qf_copy(i, xpeer).wait_recv()
+
+    pass_queries(0)
+    have_queries(0)
     KB = CAP + 16
-    nothing = jnp.zeros((QR, HD), bf)
     scale = HD ** (-0.5)
 
-    def sides(block):
-        return (
-            jnp.concatenate([block[:, 0:HD], block[:, 2 * HD:3 * HD]], 1),
-            jnp.concatenate([block[:, HD:2 * HD], block[:, 3 * HD:4 * HD]], 1),
-        )
-
-    def attend(sh):
+    def attend(g, sh):
+        at = g * 2 * HD
         everything = []
         for n in range(SG):
             i = sh * SG + n
-            rows = gq[holders[i]]
-            wide = jnp.concatenate(
-                [
-                    jnp.concatenate([rows[:QR], nothing], 1),
-                    jnp.concatenate([nothing, rows[QR:]], 1),
-                ],
-                0,
-            )
-            fresh = gkv[holders[i]].astype(f32)
+            rows = gq[g][holders[i]]
+            fresh = gkv[g][holders[i]].astype(f32)
             fresh = jnp.concatenate(
                 [fresh, jnp.zeros((KB - CAP - STEPS, fresh.shape[1]), f32)], 0
             ).astype(bf)
-            new_keys, new_values = sides(fresh)
-            keys, values = sides(wd_v.at[i // per, kept_rows(i)])
-            keys = jnp.concatenate([keys, new_keys], 0)
+            kept = kept_rows(i)
+            keys = jnp.concatenate([wd_v[i // per, kept, at:at + HD], fresh[:, :HD]], 0)
             scores = lax.dot_general(
-                wide, keys, (((1,), (1,)), ((), ())), preferred_element_type=f32
+                rows, keys, (((1,), (1,)), ((), ())), preferred_element_type=f32
             )
-            everything.append((scores, values, new_values))
+            everything.append((scores, fresh[:, HD:]))
         weighted = []
         for n in range(SG):
-            scores, values, new_values = everything[n]
+            scores = everything[n][0]
             length = lengths[sh * SG + n]
             column = lax.broadcasted_iota(jnp.int32, scores.shape, 1)
-            step = (lax.broadcasted_iota(jnp.int32, scores.shape, 0) // groups) % STEPS
+            step = lax.broadcasted_iota(jnp.int32, scores.shape, 0) // groups
             seen = (column < length) | ((column >= CAP) & (column <= CAP + step))
             scores = jnp.where(seen, scores * scale, -jnp.inf)
             weights = jnp.exp(scores - jnp.max(scores, -1, keepdims=True))
             total = jnp.sum(weights, -1, keepdims=True)
             weighted.append((weights / total).astype(bf))
         for n in range(SG):
-            values = jnp.concatenate(everything[n][1:], 0)
-            mixed = jnp.dot(weighted[n], values, preferred_element_type=f32)
-            for g in range(kv_local):
-                at = (n * kv_local + g) * QR
-                of[at:at + QR, :] = mixed[g * QR:(g + 1) * QR, g * HD:(g + 1) * HD]
-
-    def t_copy(sh, ss_, rs_, block, peer):
-        return remote(tb.at[sh, block], tb.at[sh, block], ss_.at[sh], rs_.at[sh], "att", peer)
+            i = sh * SG + n
+            kept = kept_rows(i)
+            values = jnp.concatenate(
+                [wd_v[i // per, kept, at + HD:at + 2 * HD], everything[n][1]], 0
+            )
+            of[n * QR:(n + 1) * QR, :] = jnp.dot(
+                weighted[n], values, preferred_element_type=f32
+            )
 
     heads = T // HD
-    for i in range(S):
-        cache_copy(i).wait()
-
-    for sh in range(2):
-        attend(sh)
-        for head in range(kv_local * groups):
-            g, j = head // groups, head % groups
-            both = [
-                of[pl.ds(g * QR + t * groups + j, SG, stride=kv_local * QR), :]
-                for t in range(STEPS)
-            ]
-            tb[sh, a, head // heads, :, (head % heads) * HD:(head % heads + 1) * HD] = (
-                jnp.concatenate(both, 0).astype(bf)
-            )
-        t_copy(sh, tx_ss, tx_rs, a, xpeer).start()
-        t_copy(sh, tp_ss, tp_rs, a, partner).start()
-
+    chunks = groups // heads
+
+    def t_copy(g, sh, ss_, rs_, block, peer):
+        part = tb.at[sh, block, pl.ds(g * chunks, chunks)]
+        at = g * 2 + sh if peer is far else 0
+        return remote(part, part, ss_.at[0], rs_.at[at], "att", peer)
+
+    def t_all(ss_, rs_, block, peer):
+        return remote(tb.at[:, block], tb.at[:, block], ss_.at[0], rs_.at[0], "att", peer)
+
+    for g in range(kv_local):
+        if g > 0:
+            have_queries(g)
+        for sh in range(2):
+            if g == 0:
+                for n in range(SG):
+                    cache_copy(sh * SG + n).wait()
+            attend(g, sh)
+            if sh == 0 and g + 1 < kv_local:
+                pass_queries(g + 1)
+            for j in range(groups):
+                both = [
+                    of[pl.ds(t * groups + j, SG, stride=QR), :] for t in range(STEPS)
+                ]
+                tb[sh, a, g * chunks + j // heads, :, (j % heads) * HD:(j % heads + 1) * HD] = (
+                    jnp.concatenate(both, 0).astype(bf)
+                )
+            t_copy(g, sh, tx_ss, tx_rs, a, far).start()
+            t_copy(g, sh, tp_ss, tp_rs, a, partner).start()
+
+    pieces = [(g, sh) for g in range(kv_local) for sh in range(2)]
     for k in range(NA):
         wcopy(wd, wd_v, wd_s, k).start()
-    for sh in range(2):
-        t_copy(sh, tx_ss, tx_rs, xpeer, xpeer).wait_recv()
-        t_copy(sh, tf_ss, tf_rs, xpeer, partner).start()
+    for g, sh in pieces:
+        t_copy(g, sh, tx_ss, tx_rs, far, far).wait_recv()
+        t_copy(g, sh, tf_ss, tf_rs, far, partner).start()
     sq[...] = jnp.zeros_like(sq)
     in_copy.wait()
 
@@ -290,26 +307,21 @@
                 block = kept_in[at:at + BR // STEPS, :, k * TK:(k + 1) * TK]
                 res[j, owner * BR:(owner + 1) * BR, :] = block.reshape(BR, TK)
 
-    for sh in range(2):
-        t_copy(sh, tp_ss, tp_rs, partner, partner).wait_recv()
-        t_copy(sh, tf_ss, tf_rs, far, partner).wait_recv()
+    t_all(tp_ss, tp_rs, partner, partner).wait_recv()
+    t_all(tf_ss, tf_rs, xpeer, partner).wait_recv()
     for k in range(NA):
         attended[:, k * T:(k + 1) * T] = lax.dot_general(
             place[...], tb[:, :, k].reshape(2 * HR, T), (((0,), (0,)), ((), ())),
             preferred_element_type=f32,
         ).astype(bf)
 
-    for i in range(2):
-        t_copy(i, tx_ss, tx_rs, a, xpeer).wait_send()
-        t_copy(i, tp_ss, tp_rs, a, partner).wait_send()
-        t_copy(i, tf_ss, tf_rs, xpeer, partner).wait_send()
     @pl.loop(0, NK)
     def _(k):
         parts = T // TK
 
         @pl.when(k % parts == 0)
         def _():
-            wcopy(wo, wo_v, wo_s, k // parts).wait()
+            wcopy(wo, wo_v, wo_s, k // parts, k // parts).wait()
 
         at = pl.ds(pl.multiple_of((k % parts) * TK, TK), TK)
         p = jnp.dot(attended[...], wo_v[k // parts, :, at], preferred_element_type=f32).astype(bf)
@@ -375,22 +387,24 @@
                 acc[e, k] += p.reshape(acc.shape[2:])
         for k in ks:
             for e in range(2):
-                for xx in range(2):
-                    s1[hh * NF + k, e, xx] = acc[e, k, 2 * xx + (1 - c)].astype(bf)
+                for at, owner in enumerate((partner, xpeer)):
+                    s1[hh * NF + k, e, at] = acc[e, k, owner].astype(bf)
             c1_copy(hh, k).start()
 
     def second(hh, k):
         c1_copy(hh, k).wait_recv()
         j = hh * NF + k
         for e in range(2):
-            s2[j, e] = (acc[e, k, xpeer] + r1[j, e, 1 - x].astype(f32)).astype(bf)
-            o2[j, e] = acc[e, k, a] + r1[j, e, x].astype(f32)
+            s2[j, e] = (acc[e, k, far] + r1[j, e, 1].astype(f32)).astype(bf)
+            o2[j, e] = acc[e, k, a] + r1[j, e, 0].astype(f32)
         c2_copy(hh, k).start()
 
     def inverse_of(hh):
+        remote(
+            ss.at[hh, pl.ds(0, A - 1)], ssr.at[hh], q_ss.at[0], q_rs.at[hh], "att", partner
+        ).wait_recv()
         total_squares = ss[hh, a]
         for d in range(1, A):
-            q_copy(hh, d).wait_recv()
             total_squares = total_squares + ssr[hh, d - 1]
         inv[hh] = lax.rsqrt(total_squares / D + epsilon)
 
@@ -405,12 +419,16 @@
         hp_copy(hh, k, a).start()
 
     def fourth(hh, k):
-        hx_copy(hh, k, xpeer).wait_recv()
-        hf_copy(hh, k, xpeer).start()
+        hx_copy(hh, k, far).wait_recv()
+        hf_copy(hh, k, far).start()
 
     def fifth(hh, k):
         hp_copy(hh, k, partner).wait_recv()
-        hf_copy(hh, k, far).wait_recv()
+        hf_copy(hh, k, xpeer).wait_recv()
+
+    def h_all(block, count, ss_, rs_, peer):
+        part = hb.at[pl.ds(0, count), block]
+        return remote(part, part, ss_.at[0], rs_.at[0], "att", peer)
 
     def down_chunk(hh, n, k):
         at = pl.ds(pl.multiple_of(k * T, T), T)
@@ -424,10 +442,8 @@
 
     late = min(2, NF)
 
-    @pl.loop(0, NF)
-    def _(k):
-        wcopy(wg, wg_v, wg_s, k).wait()
-        wcopy(wu, wu_v, wu_s, k).wait()
+    wait_bytes(wg_v, wg_s.at[0])
+    wait_bytes(wu_v, wu_s.at[0])
 
     def advance(hh, i, fresh=False):
         normed(hh, i)
@@ -534,13 +550,14 @@
         fourth(0, k)
     inverse_of(1)
 
-    @pl.loop(0, NF)
-    def _(k):
-        fifth(0, k)
-
+    h_all(partner, NF, hp_ss, hp_rs, partner).wait_recv()
+    h_all(xpeer, NF, hf_ss, hf_rs, partner).wait_recv()
+
+    t_all(tx_ss, tx_rs, a, far).wait_send()
+    t_all(tp_ss, tp_rs, a, partner).wait_send()
+    t_all(tf_ss, tf_rs, far, partner).wait_send()
     share = -(-NF // NA)
-    for n in range(NA):
-        wcopy(wd, wd_v, wd_s, n).wait()
+    wait_bytes(wd_v, wd_s.at[0])
 
     @pl.loop(0, NA)
     def _(n):
@@ -584,55 +601,59 @@
         acc[0, n] += down_chunk(1, n, NF - 1).reshape(acc.shape[2:])
         down_send(1, n)
 
+    def d_all(part, at):
+        return remote(part, part, d_ss.at[0], d_rs.at[at], "ffn", (z + 1) % Z)
+
+    def out_copy(hh, n):
+        j = hh * NA + n
+        to = out.at[pl.ds(hh * BR, BR), pl.ds(n * T, T)]
+        return pltpu.make_async_copy(result.at[j], to, out_s.at[0])
+
     for hh in range(2):
         for n in range(NA):
             j = hh * NA + n
+            if hh == 0 and n == 0:
+                d_all(rd.at[pl.ds(0, NA)], 0).wait_recv()
+            if hh > 0:
+                d_all(rd.at[j], 1 + n).wait_recv()
             total = acc[1 - hh, n, z]
             for d in range(1, Z):
-                d_copy(hh, n, d).wait_recv()
                 total = total + rd[j, d - 1].astype(f32)
             mine = pl.ds(pl.multiple_of(z * BR, BR), BR)
             parts = T // TK
             kept = [res[hh * NK + n * parts + e, mine, :].astype(f32) for e in range(parts)]
             total = total + jnp.concatenate(kept, -1)
-            at = hh * (BR // STEPS)
-            out[at:at + BR // STEPS, :, n * T:(n + 1) * T] = total.reshape(
-                BR // STEPS, STEPS, T
-            ).astype(bf)
-
-    for hh in range(2):
-        for n in range(NA):
-            for d in range(1, Z):
-                d_copy(hh, n, d).wait_send()
+            result[j] = total.astype(bf)
+            out_copy(hh, n).start()
+
+    wait_bytes(result, out_s.at[0])
+    for d in range(1, Z):
+        peer = (z + d) % Z
+        sent = tb.at[:, peer]
+        remote(sent, sent, d_ss.at[d - 1], d_rs.at[0], "ffn", peer).wait_send()
 
     @pl.when(inside == 0)
     def _():
-        @pl.loop(0, NT)
-        def _(j):
-            a_copy(j, inner).wait_send()
+        remote(pa, ra, a_ss.at[0], a_rs.at[0], "ffn", inner).wait_send()
 
     @pl.when(inside > 0)
     def _():
-        @pl.loop(0, NT)
-        def _(j):
-            m_copy(j).wait_send()
-            n_copy(j, outer).wait_send()
-
-    for hh in range(2):
-        for d in range(1, A):
-            q_copy(hh, d).wait_send()
-    for i in range(2):
+        remote(pa, rm, m_ss.at[0], m_rs.at[0], "ffn", other).wait_send()
+        remote(res, res, n_ss.at[0], n_rs.at[0], "ffn", outer).wait_send()
+
+    for d in range(1, A):
+        peer = (a + d) % A
+        sent = ss.at[:, peer]
+        remote(sent, ssr.at[:, d - 1], q_ss.at[d - 1], q_rs.at[0], "att", peer).wait_send()
+    for i in range(2 * kv_local):
         qx_copy(i, a).wait_send()
         qp_copy(i, a).wait_send()
-        qf_copy(i, xpeer).wait_send()
-    for hh in range(2):
-        @pl.loop(0, NF)
-        def _(k):
-            c1_copy(hh, k).wait_send()
-            c2_copy(hh, k).wait_send()
-            hp_copy(hh, k, a).wait_send()
-            hx_copy(hh, k, a).wait_send()
-            hf_copy(hh, k, xpeer).wait_send()
+        qf_copy(i, far).wait_send()
+    remote(s1, r1, c1_ss.at[0], c1_rs.at[0], "att", partner).wait_send()
+    remote(s2, r2, c2_ss.at[0], c2_rs.at[0], "att", far).wait_send()
+    h_all(a, 2 * NF, hp_ss, hp_rs, partner).wait_send()
+    h_all(a, 2 * NF, hx_ss, hx_rs, far).wait_send()
+    h_all(far, 2 * NF, hf_ss, hf_rs, partner).wait_send()
 
 
 def fused(slots, lengths, q, kv, incoming, gain, cache, w_out, w_gate, w_up, w_down):
@@ -647,6 +668,7 @@
     NA, NK, NF = width // T, width // TK, units // T
     AB = rows // 4
     S = cache.shape[0]
+    KG = cache.shape[2] // (2 * HD)
     bf, f32 = jnp.bfloat16, jnp.float32
     V = pltpu.VMEM
     dma = pltpu.SemaphoreType.DMA
@@ -655,7 +677,8 @@
     hbm = pl.BlockSpec(memory_space=pl.ANY)
     scratch = [
         pltpu.SMEM((S,), jnp.int32), V((rows, rows), bf), V(incoming.shape, bf),
-        V((4 * S, STEPS * q.shape[2] // HD, HD), bf), V((4 * S,) + kv.shape[1:], bf),
+        V((4 * S, STEPS * H // KVH, HD), bf), V((4 * S, STEPS, 2 * HD), bf),
+        V((4 * S, STEPS * H // KVH, HD), bf), V((4 * S, STEPS, 2 * HD), bf),
         V((S * STEPS * q.shape[2] // HD, HD), f32), V((S * STEPS, HD), f32),
         V((2, 4, kdim // T, AB // 2, T), bf), V((rows, kdim), bf),
         V((NA, kdim, T), bf), V((NF, width, T), bf), V((NF, width, T), bf), V((NA, units, T), bf),
@@ -665,17 +688,20 @@
         V((2, NF, 4, BR, T), f32), V((2 * NF, 2, 2, BR, T), bf),
         V((2 * NF, 2, 2, BR, T), bf), V((2 * NF, 2, BR, T), bf), V((2 * NF, 2, BR, T), f32),
         V((2 * NF, 2, BR, T), bf), V((2 * NF, 4, BR, T), bf),
-        V((2 * NA, Z - 1, BR, T), bf),
-        dma((NA,)), dma((NF,)), dma((NF,)), dma((NA,)),
-        dma((1,)),
-    ] + [dma((2 * NK,)) for _ in range(6)] + [dma((6,)), dma((6,))]
-    scratch += [dma((2 * NF,)) for _ in range(10)] + [dma((2 * NA, Z - 1)), dma((2 * NA, Z - 1))]
-    scratch += [dma((S,))] + [dma((2,)) for _ in range(6)] + [dma((2,)) for _ in range(6)]
+        V((2 * NA, Z - 1, BR, T), bf), V((2 * NA, BR, T), bf), dma((1,)),
+        dma((NA,)), dma((1,)), dma((1,)), dma((1,)), dma((1,)),
+        dma((1,)), dma((2 * NK,)), dma((1,)), dma((2 * NK,)), dma((1,)), dma((2 * NK,)), dma((3,)), dma((2,)),
+        dma((1,)), dma((2 * NF,)), dma((1,)), dma((2 * NF,)),
+        dma((1,)), dma((1 + NF,)), dma((1,)), dma((2 * NF,)), dma((1,)), dma((1 + NF,)),
+        dma((3,)), dma((1 + NA,)),
+        dma((S,)), dma((4,)), dma((4,)), dma((4,)), dma((4,)), dma((4,)), dma((4,)),
+        dma((1,)), dma((1,)), dma((1,)), dma((2 * KG,)), dma((1,)), dma((1,)),
+    ]
     return pl.pallas_call(
         functools.partial(layer_kernel, (Z, HR, BR, T, TK, NA, NK, NF)),
-        out_shape=jax.ShapeDtypeStruct((rows // Z // STEPS, STEPS, width), bf),
+        out_shape=jax.ShapeDtypeStruct((rows // Z, width), bf),
         in_specs=[sm, vm, sm, vm, vm, hbm, vm, hbm, hbm, hbm, hbm, hbm],
-        out_specs=vm,
+        out_specs=hbm,
         scratch_shapes=scratch,
         compiler_params=pltpu.CompilerParams(
             collective_id=1, has_side_effects=True, vmem_limit_bytes=67043328
@@ -704,7 +730,7 @@
 def local_fused(
     incoming, queries, new_kv, cache, lengths, slot_of, w_out, norm_gain, w_gate, w_up, w_down
 ):
-    return fused(
+    out = fused(
         slot_of,
         lengths,
         queries,
@@ -717,6 +743,7 @@
         w_up,
         w_down,
     )
+    return out.reshape(-1, STEPS, out.shape[1])
 
 
 def local(

time: 70.3 us -> 67.2 us (0.956)
  Pallas kernels: 68.5 us -> 65.4 us
    pallas_call x1, Pallas kernels: 68.5 us -> 65.4 us  [fused(): pl.pallas_call(functools.partial(layer_kernel, (Z, HR, BR, T, TK, NA, NK,...]
    reshape x0 -> x1, local copies, waits for them, and re-layouts: none -> 1.66 us  [local_fused(): return out.reshape(-1, STEPS, out.shape[1])]
    unnamed x1 -> x0, local copies, waits for them, and re-layouts: 1.65 us -> none
where the time goes in v4:
time: 67.2 us; the launch traced here: 67.1 us
  Pallas kernels  65.4 us (97%)
  local copies, waits for them, and re-layouts  1.66 us (2%)
    pallas_call x1, Pallas kernels, fused(): pl.pallas_call(functools.partial(layer_kernel, (Z, HR, BR, T, TK, NA, NK,...  65.4 us
    reshape x1, local copies, waits for them, and re-layouts, local_fused(): return out.reshape(-1, STEPS, out.shape[1])  1.66 us

profile of v4, /device:TPU:0, one launch (start us, length us, event | category | flops | bytes accessed | tf_op | source)
XLA Modules:
  0.0 67.1 jit_solution(4532079446848191178)
XLA Ops:
  0.0 65.4 %shard_map.109 = bf16[32,2048]{1,0:T(8,128)(2,1)} custom-call(s32[64]{0:T(128)} %slots.1, s32[1,64]{1,0:T(1,128)} %bitcast.3, s32[16]{0:T(128)} %lengths.1, bf16[16,2,2048]{2,1,0:T(2,128)(2,1)} %q.1, bf16[16,2,512]{2,1,0:T(2,128)(2,1)} %kv.1, bf16[64,2,2048]{2,1,0:T(2,128)(2,1)} %incoming.1, f32[1,2048]{1,0:T(1,128)} %bitcast.2, ...), custom_call_target="tpu_custom_call" | custom-call | tf_op jit(solution)/shard_map/pallas_call | solution.py:700
  65.4 1.7 %reshape.3 = bf16[16,2,2048]{2,1,0:T(2,128)(2,1)} reshape(bf16[32,2048]{1,0:T(8,128)(2,1)} %shard_map.109) | data formatting | bytes 262144 | tf_op jit(solution)/shard_map/reshape | solution.py:746

commit v5 on v4

--- a/solution.py
+++ b/solution.py
@@ -26,7 +26,7 @@
     wo_v, wg_v, wu_v, wd_v,
     pa, ra, rm, res, h, sq, inv, ss, ssr,
     acc, s1, r1, s2, o2, r2, hb,
-    rd, result, out_s,
+    rd,
     wo_s, wg_s, wu_s, wd_s,
     in_s, a_ss, a_rs, m_ss, m_rs, n_ss, n_rs, q_ss, q_rs,
     c1_ss, c1_rs, c2_ss, c2_rs,
@@ -604,11 +604,6 @@
     def d_all(part, at):
         return remote(part, part, d_ss.at[0], d_rs.at[at], "ffn", (z + 1) % Z)
 
-    def out_copy(hh, n):
-        j = hh * NA + n
-        to = out.at[pl.ds(hh * BR, BR), pl.ds(n * T, T)]
-        return pltpu.make_async_copy(result.at[j], to, out_s.at[0])
-
     for hh in range(2):
         for n in range(NA):
             j = hh * NA + n
@@ -623,10 +618,8 @@
             parts = T // TK
             kept = [res[hh * NK + n * parts + e, mine, :].astype(f32) for e in range(parts)]
             total = total + jnp.concatenate(kept, -1)
-            result[j] = total.astype(bf)
-            out_copy(hh, n).start()
-
-    wait_bytes(result, out_s.at[0])
+            out[hh * BR:(hh + 1) * BR, n * T:(n + 1) * T] = total.astype(bf)
+
     for d in range(1, Z):
         peer = (z + d) % Z
         sent = tb.at[:, peer]
@@ -688,7 +681,7 @@
         V((2, NF, 4, BR, T), f32), V((2 * NF, 2, 2, BR, T), bf),
         V((2 * NF, 2, 2, BR, T), bf), V((2 * NF, 2, BR, T), bf), V((2 * NF, 2, BR, T), f32),
         V((2 * NF, 2, BR, T), bf), V((2 * NF, 4, BR, T), bf),
-        V((2 * NA, Z - 1, BR, T), bf), V((2 * NA, BR, T), bf), dma((1,)),
+        V((2 * NA, Z - 1, BR, T), bf),
         dma((NA,)), dma((1,)), dma((1,)), dma((1,)), dma((1,)),
         dma((1,)), dma((2 * NK,)), dma((1,)), dma((2 * NK,)), dma((1,)), dma((2 * NK,)), dma((3,)), dma((2,)),
         dma((1,)), dma((2 * NF,)), dma((1,)), dma((2 * NF,)),
@@ -699,12 +692,12 @@
     ]
     return pl.pallas_call(
         functools.partial(layer_kernel, (Z, HR, BR, T, TK, NA, NK, NF)),
-        out_shape=jax.ShapeDtypeStruct((rows // Z, width), bf),
+        out_shape=pltpu.VMEM((rows // Z, width), bf),
         in_specs=[sm, vm, sm, vm, vm, hbm, vm, hbm, hbm, hbm, hbm, hbm],
-        out_specs=hbm,
+        out_specs=vm,
         scratch_shapes=scratch,
         compiler_params=pltpu.CompilerParams(
-            collective_id=1, has_side_effects=True, vmem_limit_bytes=67043328
+            collective_id=1, has_side_effects=True, vmem_limit_bytes=65500000
         ),
     )(slots, slots[None], lengths, q, kv, incoming, gain, cache, w_out, w_gate, w_up, w_down)
 

time: 67.2 us -> 65.7 us (0.978)
  local copies, waits for them, and re-layouts: 1.66 us -> 0.76 us
    reshape x1, local copies, waits for them, and re-layouts: 1.66 us -> 0.76 us  [local_fused(): return out.reshape(-1, STEPS, out.shape[1])]
where the time goes in v5:
time: 65.7 us; the launch traced here: 65.6 us
  Pallas kernels  64.8 us (99%)
  local copies, waits for them, and re-layouts  0.76 us (1%)
    pallas_call x1, Pallas kernels, fused(): pl.pallas_call(functools.partial(layer_kernel, (Z, HR, BR, T, TK, NA, NK,...  64.8 us

profile of v5, /device:TPU:0, one launch (start us, length us, event | category | flops | bytes accessed | tf_op | source)
XLA Modules:
  0.0 65.6 jit_solution(13354465791798468795)
XLA Ops:
  0.0 64.8 %shard_map.109 = bf16[32,2048]{1,0:T(8,128)(2,1)S(1)} custom-call(s32[64]{0:T(128)} %slots.1, s32[1,64]{1,0:T(1,128)} %bitcast.3, s32[16]{0:T(128)} %lengths.1, bf16[16,2,2048]{2,1,0:T(2,128)(2,1)} %q.1, bf16[16,2,512]{2,1,0:T(2,128)(2,1)} %kv.1, bf16[64,2,2048]{2,1,0:T(2,128)(2,1)} %incoming.1, f32[1,2048]{1,0:T(1,128)} %bitcast.2, ...), custom_call_target="tpu_custom_call" | custom-call | tf_op jit(solution)/shard_map/pallas_call | solution.py:693
  64.8 0.8 %reshape.3 = bf16[16,2,2048]{2,1,0:T(2,128)(2,1)} reshape(bf16[32,2048]{1,0:T(8,128)(2,1)S(1)} %shard_map.109) | data formatting | bytes 262144 | tf_op jit(solution)/shard_map/reshape | solution.py:739

commit v6 on v5

--- a/solution.py
+++ b/solution.py
@@ -65,6 +65,12 @@
     def cache_copy(i):
         return pltpu.make_async_copy(cache.at[i], wd_v.at[i // per, kept_rows(i)], cache_s.at[i])
 
+    barrier = pltpu.get_barrier_semaphore()
+    for d in range(1, Z):
+        pl.semaphore_signal(barrier, 1, device_id={"ffn": (z + d) % Z}, device_id_type=MESH)
+    for d in range(1, A):
+        pl.semaphore_signal(barrier, 1, device_id={"att": (a + d) % A}, device_id_type=MESH)
+
     @pl.loop(0, S)
     def _(i):
         cache_copy(i).start()
@@ -91,11 +97,6 @@
         rows = of[g * S * QR:(g + 1) * S * QR, :]
         gq[g][pl.ds(a * S, S)] = rows.reshape((S,) + gq[g].shape[1:]).astype(bf)
         gkv[g][pl.ds(a * S, S)] = kv[:, :, g * 2 * HD:(g + 1) * 2 * HD]
-    barrier = pltpu.get_barrier_semaphore()
-    for d in range(1, Z):
-        pl.semaphore_signal(barrier, 1, device_id={"ffn": (z + d) % Z}, device_id_type=MESH)
-    for d in range(1, A):
-        pl.semaphore_signal(barrier, 1, device_id={"att": (a + d) % A}, device_id_type=MESH)
     pl.semaphore_wait(barrier, Z - 1 + A - 1)
 
     def remote(src, dst, ss_, rs_, axis, peer):

time: 65.7 us -> 65.6 us (level)
  no operation moved by 1% of the time
where the time goes in v6:
time: 65.6 us; the launch traced here: 65.5 us
  Pallas kernels  64.7 us (99%)
  local copies, waits for them, and re-layouts  0.76 us (1%)
    pallas_call x1, Pallas kernels, fused(): pl.pallas_call(functools.partial(layer_kernel, (Z, HR, BR, T, TK, NA, NK,...  64.7 us

profile of v6, /device:TPU:0, one launch (start us, length us, event | category | flops | bytes accessed | tf_op | source)
XLA Modules:
  0.0 65.5 jit_solution(3247890431369790094)
XLA Ops:
  0.0 64.7 %shard_map.109 = bf16[32,2048]{1,0:T(8,128)(2,1)S(1)} custom-call(s32[64]{0:T(128)} %slots.1, s32[1,64]{1,0:T(1,128)} %bitcast.3, s32[16]{0:T(128)} %lengths.1, bf16[16,2,2048]{2,1,0:T(2,128)(2,1)} %q.1, bf16[16,2,512]{2,1,0:T(2,128)(2,1)} %kv.1, bf16[64,2,2048]{2,1,0:T(2,128)(2,1)} %incoming.1, f32[1,2048]{1,0:T(1,128)} %bitcast.2, ...), custom_call_target="tpu_custom_call" | custom-call | tf_op jit(solution)/shard_map/pallas_call | solution.py:694
  64.7 0.8 %reshape.3 = bf16[16,2,2048]{2,1,0:T(2,128)(2,1)} reshape(bf16[32,2048]{1,0:T(8,128)(2,1)S(1)} %shard_map.109) | data formatting | bytes 262144 | tf_op jit(solution)/shard_map/reshape | solution.py:740
